TPU v7x, 32 devices: a whole 2x2x4 slice. The times are simulated.
32 devices in a mesh: groups: 2 (over x), expert: 16 (over z, y, core).
Axes of the slice: x: 2, y: 2, z: 4, core: 2. Of those that a mesh axis runs over, the one named last changes fastest.
Arguments:
- hidden_in: bfloat16 [256, 4096], P(('groups', 'expert')), parts along dimension 0, may hold values from -6 to 6
- queries: bfloat16 [256, 4096], P(('groups', 'expert')), parts along dimension 0, may hold values from -8 to 8
- decode_key_value: bfloat16 [256, 2, 256], P(('groups', 'expert')), parts along dimension 0, may hold values from -6 to 6
- local_kv: bfloat16 [1024, 2, 16, 256], P(('groups', 'expert')), parts along dimension 0, may hold values from -8 to 8
- page_table: int32 [256, 16], P(('groups', 'expert')), parts along dimension 0, may hold values from 0 to 31
- seq_blocks: int32 [256], P(('groups', 'expert')), parts along dimension 0, may hold values from 1 to 16
- prompt_kv: bfloat16 [32, 16, 2, 16, 256], P(('groups', 'expert')), parts along dimension 0, may hold values from -8 to 8
- prompt_owner: int32 [32], P('groups'), parts along dimension 0, may hold values from 0 to 15, as said below
- prompt_pages: int32 [32], P('groups'), parts along dimension 0, may hold values from 1 to 16
- norm_gain: float32 [4096], replicated, may hold values from 0.5 to 1.5
- router: bfloat16 [4096, 8], replicated, may hold values from -0.09375 to 0.09375
- w_gate: bfloat16 [16, 4096, 384], P('expert'), may hold values from -0.09375 to 0.09375
- w_up: bfloat16 [16, 4096, 384], P('expert'), may hold values from -0.09375 to 0.09375
- w_down: bfloat16 [16, 384, 4096], P('expert'), may hold values from -0.21875 to 0.21875
- route_ids: int32 [256, 8], P(('groups', 'expert')), parts along dimension 0, may hold values from 0 to 7, as said below
Outputs:
- layer_out: bfloat16 [256, 4096], P(('groups', 'expert')), parts along dimension 0
There are 2 independent parts, one for each index of `groups`. A program takes and returns all parts, laid end to end along the dimension named above; an argument that names none is the same for every part. Nothing has to cross between parts.
Inputs may be any that keep to these rules, and one draw needn't show every extreme that they name: `prompt_owner`: each device is named by at most 2 prompts, and by exactly 2 for some of the devices. `route_ids`: each row names 8 different experts; among the rows of one device no expert is named more than 8 times, a bound that some block reaches. `page_table`: indices among the pages of the sequence's own device.
All inputs are finite; a program needn't handle non-finite values.
Results may differ from a plain program's by a relative error of at most 0.0056.
Values may be sent and summed in bfloat16 or wider, within the bound.
No kernel may reach another device: no remote copies, remote signals or barrier semaphores. Data moves between devices by JAX's collectives and lax.ppermute only.
A program may use at most 128 MiB of HBM per device.

v0:
```python
import math

import jax
import jax.numpy as jnp
from jax import lax
from jax.sharding import PartitionSpec as P

D = 4096
QUERY_HEADS = 32
KEY_VALUE_HEADS = 2
HEAD_SIZE = 128
PAGE_TOKENS = 16
TOPK = 8
MAXB = 16
MAXP = 2


norm_eps = 1e-06
masked_score = -1e30


def partner(x, axis, apart):
    return lax.ppermute(x, axis, [(i, i ^ 1 << apart) for i in range(lax.axis_size(axis))])


def attend(rows_of_queries, rows_of_keys, rows_of_values, allowed, token_own_key, token_own_value):
    decode_tokens = rows_of_queries.shape[0]
    heads_of_queries = rows_of_queries.reshape(
        decode_tokens, KEY_VALUE_HEADS, QUERY_HEADS // KEY_VALUE_HEADS, HEAD_SIZE
    )
    heads_of_keys = rows_of_keys.reshape(decode_tokens, -1, KEY_VALUE_HEADS, HEAD_SIZE)
    heads_of_values = rows_of_values.reshape(decode_tokens, -1, KEY_VALUE_HEADS, HEAD_SIZE)
    scale_for_scores = 1.0 / math.sqrt(HEAD_SIZE)
    allowed_mask = allowed[:, None, None, :]
    scores = (
        jnp.einsum(
            "tkgd,tlkd->tkgl", heads_of_queries, heads_of_keys, preferred_element_type=jnp.float32
        )
        * scale_for_scores
    )
    scores = jnp.where(allowed_mask, scores, masked_score)
    token_own_score = (
        jnp.einsum(
            "xejp,xep->xej",
            heads_of_queries,
            token_own_key.reshape(decode_tokens, KEY_VALUE_HEADS, HEAD_SIZE),
            preferred_element_type=jnp.float32,
        )
        * scale_for_scores
    )
    peak = jnp.maximum(jnp.max(scores, -1), token_own_score)
    weights = jnp.where(allowed_mask, jnp.exp(scores - peak[..., None]), 0.0)
    own_weight = jnp.exp(token_own_score - peak)
    denominator = jnp.sum(weights, -1) + own_weight
    probs = (weights / denominator[..., None]).astype(jnp.bfloat16)
    token_own_probability = (own_weight / denominator).astype(jnp.bfloat16)
    blended_noise = jnp.einsum(
        "tkgl,tlkd->tkgd", probs, heads_of_values, preferred_element_type=jnp.float32
    )
    blended_noise = blended_noise + token_own_probability.astype(jnp.float32)[
        ..., None
    ] * token_own_value.reshape(decode_tokens, KEY_VALUE_HEADS, 1, HEAD_SIZE).astype(jnp.float32)
    return blended_noise.reshape(decode_tokens, QUERY_HEADS * HEAD_SIZE).astype(jnp.bfloat16)


def local(
    hidden_in,
    queries,
    decode_key_value,
    local_kv,
    page_table,
    seq_blocks,
    prompt_kv,
    prompt_owner,
    prompt_pages,
    norm_gain,
    router,
    w_gate,
    w_up,
    w_down,
    route_ids,
):
    devices = lax.axis_size("expert")
    position = lax.axis_index("expert")
    experts = devices // 2
    seq_dev = hidden_in.shape[0]
    key_value_width = KEY_VALUE_HEADS * HEAD_SIZE
    capacity = min(seq_dev, max(2, 2 * ((3 * seq_dev * TOPK + 2 * devices - 1) // (2 * devices))))
    half_cap = capacity // 2
    even_core = position % 2 == 0
    prompt_count = prompt_owner.shape[0]
    prompt_range = jnp.arange(prompt_count, dtype=jnp.int32)
    same_owner = prompt_owner[:, None] == prompt_owner[None, :]
    earlier = prompt_range[None, :] < prompt_range[:, None]
    arrival = jnp.sum((same_owner & earlier).astype(jnp.int32), 1)
    matching = (
        prompt_owner[None, None, :] == jnp.arange(devices, dtype=jnp.int32)[:, None, None]
    ) & (arrival[None, None, :] == jnp.arange(MAXP, dtype=jnp.int32)[None, :, None])
    chosen_prompt = jnp.sum(jnp.where(matching, prompt_range[None, None, :], 0), -1)
    occupied = jnp.any(matching, -1)
    own_picks = lax.dynamic_index_in_dim(chosen_prompt, position, 0, keepdims=False)
    own_occupied = lax.dynamic_index_in_dim(occupied, position, 0, keepdims=False)
    page_rows = prompt_kv[0]
    outgoing = jnp.take(page_rows, chosen_prompt.T.reshape(-1), axis=0).reshape(
        MAXP, devices, 2, PAGE_TOKENS, key_value_width
    )
    outgoing = jnp.where(occupied.T[:, :, None, None, None], outgoing, 0)
    arrived = lax.all_to_all(outgoing, "expert", split_axis=1, concat_axis=1, tiled=True)
    lengths = jnp.take(prompt_pages, own_picks)
    new_keys = arrived[:, :, 0].reshape(MAXP, devices * PAGE_TOKENS, key_value_width)
    new_values = arrived[:, :, 1].reshape(MAXP, devices * PAGE_TOKENS, key_value_width)
    new_allowed = (jnp.arange(devices * PAGE_TOKENS, dtype=jnp.int32) // PAGE_TOKENS)[
        None, :
    ] < lengths[:, None]
    fresh_rows = attend(
        queries[:MAXP],
        new_keys,
        new_values,
        new_allowed,
        decode_key_value[:MAXP, 0],
        decode_key_value[:MAXP, 1],
    )
    fetched = local_kv[page_table]
    old_keys = fetched[:, :, 0].reshape(seq_dev, MAXB * PAGE_TOKENS, key_value_width)
    old_values = fetched[:, :, 1].reshape(seq_dev, MAXB * PAGE_TOKENS, key_value_width)
    old_allowed = (jnp.arange(MAXB * PAGE_TOKENS, dtype=jnp.int32) // PAGE_TOKENS)[
        None, :
    ] < seq_blocks[:, None]
    old_out = attend(
        queries, old_keys, old_values, old_allowed, decode_key_value[:, 0], decode_key_value[:, 1]
    )
    new_count = jnp.sum(own_occupied.astype(jnp.int32))
    is_new = jnp.arange(MAXP, dtype=jnp.int32) < new_count
    attention = jnp.concatenate(
        [jnp.where(is_new[:, None], fresh_rows, old_out[:MAXP]), old_out[MAXP:]], 0
    )
    residual = (hidden_in.astype(jnp.float32) + attention.astype(jnp.float32)).astype(jnp.bfloat16)
    resid_wide = residual.astype(jnp.float32)
    normed = (
        resid_wide
        * lax.rsqrt(jnp.mean(resid_wide * resid_wide, -1, keepdims=True) + norm_eps)
        * norm_gain
    ).astype(jnp.bfloat16)
    logits = jnp.dot(normed, router, preferred_element_type=jnp.float32)
    expert_onehot = route_ids[:, :, None] == jnp.arange(experts, dtype=jnp.int32)[None, None, :]
    selected = jnp.sum(jnp.where(expert_onehot, logits[:, None, :], 0.0), -1)
    gate_weights = jax.nn.softmax(selected, -1)
    assigned = seq_dev * TOPK
    expert_ids = route_ids.reshape(assigned)
    chosen = (expert_ids[:, None] == jnp.arange(experts, dtype=jnp.int32)[None, :]).astype(
        jnp.int32
    )
    before = jnp.cumsum(chosen, 0) - chosen
    slot_rank = jnp.sum(before * chosen, 1)
    slot_index = expert_ids * capacity + slot_rank
    placing = slot_index[None, :] == jnp.arange(experts * capacity, dtype=jnp.int32)[:, None]
    selector = jnp.any(placing.reshape(experts * capacity, seq_dev, TOPK), -1).astype(jnp.bfloat16)
    gathered_rows = jnp.dot(selector, normed, preferred_element_type=jnp.float32).astype(
        jnp.bfloat16
    )
    outgoing_half = gathered_rows.reshape(devices, half_cap, D)
    own_half = lax.all_to_all(outgoing_half, "expert", split_axis=0, concat_axis=0, tiled=True)
    partner_half = partner(own_half, "expert", 0)
    received = jnp.where(
        even_core,
        jnp.concatenate([own_half, partner_half], 1),
        jnp.concatenate([partner_half, own_half], 1),
    )
    flattened = received.reshape(devices * capacity, D)
    gate_proj = jnp.dot(flattened, w_gate[0], preferred_element_type=jnp.float32)
    up_proj = jnp.dot(flattened, w_up[0], preferred_element_type=jnp.float32)
    activated = (jax.nn.silu(gate_proj) * up_proj).astype(jnp.bfloat16)
    partial_value = jnp.dot(activated, w_down[0], preferred_element_type=jnp.float32).reshape(
        devices, capacity, D
    )
    kept = jnp.where(even_core, partial_value[:, :half_cap], partial_value[:, half_cap:])
    handed = jnp.where(even_core, partial_value[:, half_cap:], partial_value[:, :half_cap])
    partner_part = partner(handed, "expert", 0)
    finished = (kept + partner_part).astype(jnp.bfloat16)
    returned = lax.all_to_all(finished, "expert", split_axis=0, concat_axis=0, tiled=True)
    expert_sum = returned.reshape(experts * capacity, D)
    picked = jnp.take(expert_sum, slot_index, axis=0).astype(jnp.float32).reshape(seq_dev, TOPK, D)
    expert_mix = jnp.sum(picked * gate_weights[:, :, None], 1)
    return (resid_wide + expert_mix).astype(jnp.bfloat16)


def solution(mesh):
    return jax.shard_map(
        local,
        mesh=mesh,
        in_specs=(
            P(("groups", "expert"), None),
            P(("groups", "expert"), None),
            P(("groups", "expert"), None, None),
            P(("groups", "expert"), None, None, None),
            P(("groups", "expert"), None),
            P(("groups", "expert")),
            P(("groups", "expert"), None, None, None, None),
            P("groups"),
            P("groups"),
            P(),
            P(),
            P("expert", None, None),
            P("expert", None, None),
            P("expert", None, None),
            P(("groups", "expert"), None),
        ),
        out_specs=P(("groups", "expert"), None),
        check_vma=False,
    )
```

profile of v0, /device:TPU:0, one launch (start us, length us, event | category | flops | bytes accessed | tf_op | source)
XLA Modules:
  0.0 109.9 jit_solution(15105723009639426284)
XLA Ops:
  2.0 2.3 %gather_fusion.1 = bf16[32,2,16,256]{3,2,1,0:T(8,128)(2,1)} fusion(bf16[16,2,16,256]{3,2,1,0:T(8,128)(2,1)} %bitcast.111, s32[1024]{0:T(1024)S(1)} %pad_clamp_fusion.2), kind=kCustom, calls=%fused_computation.1 | custom fusion | bytes 1048704 | tf_op jit(solution)/shard_map/jit(_take)/gather | solution.py:104
  4.4 1.2 %select_select_fusion = bf16[2,16,2,16,256]{4,3,2,1,0:T(8,128)(2,1)S(1)} fusion(bf16[2,16,2,16,256]{4,3,2,1,0:T(8,128)(2,1)} %bitcast.110, pred[2,16]{1,0:T(4,128)(4,1)S(1)} %compare_and_fusion.1, pred[2,16]{1,0:T(4,128)(4,1)S(1)} %bitcast.123), kind=kLoop, calls=%fused_computation.34 | loop fusion | flops 524288 | bytes 1048640 | tf_op jit(solution)/shard_map/jit(_where)/select_n | solution.py:107
  6.4 7.5 %all-to-all-start = ((bf16[2,16,2,16,256]{4,3,0,2,1:T(8,128)(2,1)}), bf16[2,16,2,16,256]{4,3,0,2,1:T(8,128)(2,1)}, u32[]{:S(2)}, u32[]{:S(2)}) async-start(bf16[2,16,2,16,256]{4,3,0,2,1:T(8,128)(2,1)} %copy.48), calls=%async_computation | async-start | bytes 1048576 | tf_op jit(solution)/shard_map/all_to_all | solution.py:108
  14.0 3.1 %gather_fusion.2 = bf16[128,2,16,256]{3,2,1,0:T(8,128)(2,1)} fusion(bf16[32,2,16,256]{3,2,1,0:T(8,128)(2,1)} %param.18, s32[1024]{0:T(1024)S(1)} %pad_clamp_fusion.1), kind=kCustom, calls=%fused_computation.2 | custom fusion | bytes 4194816 | tf_op jit(solution)/shard_map/gather | solution.py:123
  17.1 3.0 %slice_bitcast_fusion.1 = (bf16[8,16,1,16,256]{4,3,1,0,2:T(8,128)(2,1)}, bf16[8,16,1,16,256]{4,3,1,0,2:T(8,128)(2,1)}) fusion(bf16[8,16,2,16,256]{4,3,2,1,0:T(8,128)(2,1)} %bitcast.109), kind=kLoop, calls=%fused_computation.25 | loop fusion | bytes 4194304
  20.2 2.2 %reshape_reshape_squeeze.15 = bf16[8,256,2,128]{3,2,1,0:T(2,128)(2,1)} reshape(bf16[8,16,1,16,256]{4,3,1,0,2:T(8,128)(2,1)} %get-tuple-element.10) | data formatting | bytes 2097152 | tf_op jit(solution)/shard_map/reshape;reshape;squeeze | solution.py:32
  22.4 2.2 %reshape_reshape_squeeze.14 = bf16[8,256,2,128]{3,2,1,0:T(2,128)(2,1)} reshape(bf16[8,16,1,16,256]{4,3,1,0,2:T(8,128)(2,1)} %get-tuple-element.9) | data formatting | bytes 2097152 | tf_op jit(solution)/shard_map/reshape;reshape;squeeze | solution.py:31
  24.8 1.7 %fusion.84 = (f32[8,2,16]{2,1,0:T(2,128)S(1)}, f32[8,2,16,256]{3,2,1,0:T(8,128)S(1)}) fusion(bf16[8,2,16,128]{3,0,2,1:T(8,128)(2,1)S(1)} %bitcast.127, bf16[8,256,2,128]{3,2,1,0:T(2,128)(2,1)} %reshape_reshape_squeeze.14, pred[8,256]{1,0:T(8,128)(4,1)S(1)} %broadcast_compare_fusion), kind=kOutput, calls=%fused_computation.144 | convolution fusion | flops 16973568 | bytes 1379328 | tf_op jit(solution)/shard_map/tkgd,tlkd->tkgl/dot_general | solution.py:36
  30.2 1.8 %fusion.83 = (bf16[2,16,1,16,256]{4,3,0,2,1:T(8,128)(2,1)}, bf16[2,16,1,16,256]{4,3,0,2,1:T(8,128)(2,1)S(1)}) fusion(bf16[2,16,2,16,256]{4,3,0,2,1:T(8,128)(2,1)} %all-to-all-done), kind=kLoop, calls=%fused_computation.143 | loop fusion | bytes 1048576 | tf_op jit(solution)/shard_map/slice | solution.py:110
  34.5 1.2 %fusion.85 = (f32[2,2,16]{2,1,0:T(2,128)S(1)}, f32[2,2,16,256]{3,2,1,0:T(8,128)S(1)}) fusion(bf16[2,2,16,128]{3,2,1,0:T(8,128)(2,1)S(1)} %bitcast.119, bf16[2,256,2,128]{3,2,1,0:T(2,128)(2,1)} %reshape_reshape_squeeze.12, pred[2,256]{1,0:T(4,128)(4,1)S(1)} %broadcast_compare_fusion.1), kind=kOutput, calls=%fused_computation.145 | convolution fusion | flops 4243392 | bytes 344832 | tf_op jit(solution)/shard_map/tkgd,tlkd->tkgl/dot_general | solution.py:36
  38.2 1.2 %convolution_convert_fusion = bf16[64,4096]{1,0:T(8,128)(2,1)} fusion(pred[64,8]{0,1:T(8,128)(4,1)S(1)} %fusion.54, bf16[8,4096]{1,0:T(8,128)(2,1)S(1)} %get-tuple-element.8, f32[4096]{0:T(1024)S(1)} %copy-done.5, f32[8]{0:T(128)S(1)} %add_rsqrt_fusion), kind=kOutput, calls=%fused_computation.4 | convolution fusion | flops 4587520 | bytes 606752 | tf_op jit(solution)/shard_map/dot_general | solution.py:158
  39.4 2.0 %reshape.374 = bf16[16,4,4096]{2,1,0:T(4,128)(2,1)} reshape(bf16[64,4096]{1,0:T(8,128)(2,1)} %convolution_convert_fusion) | data formatting | bytes 1048576 | tf_op jit(solution)/shard_map/reshape | solution.py:161
  41.4 20.3 %all_to_all.15 = bf16[16,4,4096]{2,1,0:T(4,128)(2,1)} all-to-all(bf16[16,4,4096]{2,1,0:T(4,128)(2,1)} %reshape.374), channel_id=1, replica_groups=mesh['groups'=2,'expert'=16] {'expert'}, dimensions={0} | all-to-all | bytes 1048576 | tf_op jit(solution)/shard_map/all_to_all | solution.py:162
  61.9 2.1 %collective-permute-done = bf16[16,4,4096]{2,1,0:T(4,128)(2,1)} collective-permute-done((bf16[16,4,4096]{2,1,0:T(4,128)(2,1)}, bf16[16,4,4096]{2,1,0:T(4,128)(2,1)}, u32[]{:S(2)}, u32[]{:S(2)}) %collective-permute-start) | collective-permute-done | bytes 524320 | tf_op jit(solution)/shard_map/ppermute | solution.py:23
  64.0 3.8 %fusion.4 = f32[128,384]{1,0:T(8,128)S(1)} fusion(bf16[1,4096,384]{2,1,0:T(8,128)(2,1)} %param.26, bf16[16,4,4096]{2,1,0:T(4,128)(2,1)} %collective-permute-done, bf16[16,4,4096]{2,1,0:T(4,128)(2,1)} %all_to_all.15, pred[]{:T(512)S(6)} %eq.103), kind=kOutput, calls=%fused_computation.9 | convolution fusion | flops 407371776 | bytes 4390913 | tf_op jit(solution)/shard_map/dot_general | solution.py:170
  67.8 5.8 %fusion = f32[16,8,4096]{2,1,0:T(8,128)} fusion(bf16[1,384,4096]{2,1,0:T(8,128)(2,1)S(1)} %copy-done, bf16[1,4096,384]{2,1,0:T(8,128)(2,1)} %param.27, f32[128,384]{1,0:T(8,128)S(1)} %fusion.4, bf16[16,4,4096]{2,1,0:T(4,128)(2,1)} %collective-permute-done, bf16[16,4,4096]{2,1,0:T(4,128)(2,1)} %all_to_all.15, pred[]{:T(512)S(6)} %eq.103), kind=kOutput, calls=%fused_computation.5 | convolution fusion | flops 810319872 | bytes 9633793 | tf_op jit(solution)/shard_map/dot_general | solution.py:173
  73.7 3.5 %slice_select_fusion = f32[16,4,4096]{2,1,0:T(4,128)} fusion(f32[16,8,4096]{2,1,0:T(8,128)} %fusion, pred[]{:T(512)S(6)} %eq.103), kind=kLoop, calls=%fused_computation.32 | loop fusion | flops 262144 | bytes 3145729 | tf_op jit(solution)/shard_map/jit(_where)/select_n | solution.py:177
  77.4 2.8 %collective-permute-done.1 = f32[16,4,4096]{2,1,0:T(4,128)} collective-permute-done((f32[16,4,4096]{2,1,0:T(4,128)}, f32[16,4,4096]{2,1,0:T(4,128)}, u32[]{:S(2)}, u32[]{:S(2)}) %collective-permute-start.1) | collective-permute-done | bytes 1048608 | tf_op jit(solution)/shard_map/ppermute | solution.py:23
  80.2 3.8 %add_convert_fusion = bf16[16,4,4096]{2,1,0:T(4,128)(2,1)} fusion(f32[16,4,4096]{2,1,0:T(4,128)} %collective-permute-done.1, f32[16,8,4096]{2,1,0:T(8,128)} %fusion, pred[]{:T(512)S(6)} %eq.103), kind=kLoop, calls=%fused_computation.31 | loop fusion | flops 786432 | bytes 3670017 | tf_op jit(solution)/shard_map/convert_element_type | solution.py:179
  83.9 4.2 %all-to-all-start.2 = ((bf16[16,4,4096]{2,1,0:T(4,128)(2,1)}), bf16[16,4,4096]{2,1,0:T(4,128)(2,1)}, u32[]{:S(2)}, u32[]{:S(2)}) async-start(bf16[16,4,4096]{2,1,0:T(4,128)(2,1)} %add_convert_fusion), calls=%async_computation.2 | async-start | bytes 1048576 | tf_op jit(solution)/shard_map/all_to_all | solution.py:180
  89.0 13.5 %all-to-all-done.2 = bf16[16,4,4096]{2,1,0:T(4,128)(2,1)} async-done(((bf16[16,4,4096]{2,1,0:T(4,128)(2,1)}), bf16[16,4,4096]{2,1,0:T(4,128)(2,1)}, u32[]{:S(2)}, u32[]{:S(2)}) %all-to-all-start.2) | async-done | bytes 524320 | tf_op jit(solution)/shard_map/all_to_all | solution.py:180
  102.5 2.0 %reshape.375 = bf16[64,4096]{1,0:T(8,128)(2,1)} reshape(bf16[16,4,4096]{2,1,0:T(4,128)(2,1)} %all-to-all-done.2) | data formatting | bytes 1048576 | tf_op jit(solution)/shard_map/reshape | solution.py:181
  104.5 3.3 %gather_fusion.3 = bf16[64,4096]{1,0:T(8,128)(2,1)} fusion(bf16[64,4096]{1,0:T(8,128)(2,1)} %reshape.375, s32[1024]{0:T(1024)S(1)} %pad_clamp_fusion), kind=kCustom, calls=%fused_computation.3 | custom fusion | bytes 1048832 | tf_op jit(solution)/shard_map/jit(_take)/gather | solution.py:182
  107.7 1.5 %multiply_reduce_fusion = f32[8,4096]{1,0:T(8,128)S(1)} fusion(bf16[64,4096]{1,0:T(8,128)(2,1)} %gather_fusion.3, f32[8,8]{1,0:T(8,128)S(1)} %fusion.63, pred[8,8]{1,0:T(8,128)(4,1)S(1)} %get-tuple-element.5), kind=kLoop, calls=%fused_computation.30 | loop fusion | flops 1015808 | bytes 655680 | tf_op jit(solution)/shard_map/reduce_sum | solution.py:183
  (87 shorter events, 13.5 us)
Async XLA Ops:
  0.0 67.8 %copy-start = (bf16[1,384,4096]{2,1,0:T(8,128)(2,1)S(1)}, bf16[1,384,4096]{2,1,0:T(8,128)(2,1)}, u32[]{:S(2)}) copy-start(bf16[1,384,4096]{2,1,0:T(8,128)(2,1)} %param.28) | copy-start | bytes 9437188
  2.0 11.9 %copy-start.7 = (s32[8,16]{1,0:T(8,128)S(1)}, s32[8,16]{1,0:T(8,128)}, u32[]{:S(2)}) copy-start(s32[8,16]{1,0:T(8,128)} %param.19) | copy-start | bytes 1540
  6.4 23.8 %all-to-all-start = ((bf16[2,16,2,16,256]{4,3,0,2,1:T(8,128)(2,1)}), bf16[2,16,2,16,256]{4,3,0,2,1:T(8,128)(2,1)}, u32[]{:S(2)}, u32[]{:S(2)}) async-start(bf16[2,16,2,16,256]{4,3,0,2,1:T(8,128)(2,1)} %copy.48), calls=%async_computation | async-start | bytes 1048576 | tf_op jit(solution)/shard_map/all_to_all | solution.py:108
  20.2 4.4 %copy-start.4 = (bf16[8,2,256]{2,1,0:T(2,128)(2,1)S(1)}, bf16[8,2,256]{2,1,0:T(2,128)(2,1)}, u32[]{:S(2)}) copy-start(bf16[8,2,256]{2,1,0:T(2,128)(2,1)} %param.17) | copy-start | bytes 24580
  20.2 4.4 %copy-start.8 = (s32[8]{0:T(128)S(1)}, s32[8]{0:T(128)}, u32[]{:S(2)}) copy-start(s32[8]{0:T(128)} %param.20) | copy-start | bytes 100
  20.2 4.5 %copy-start.6 = (bf16[8,4096]{1,0:T(8,128)(2,1)S(1)}, bf16[8,4096]{1,0:T(8,128)(2,1)}, u32[]{:S(2)}) copy-start(bf16[8,4096]{1,0:T(8,128)(2,1)} %param.16) | copy-start | bytes 196612
  24.6 2.3 %copy-start.2 = (bf16[8,256,2,128]{3,2,1,0:T(2,128)(2,1)S(1)}, bf16[8,256,2,128]{3,2,1,0:T(2,128)(2,1)}, u32[]{:S(2)}) copy-start(bf16[8,256,2,128]{3,2,1,0:T(2,128)(2,1)} %reshape_reshape_squeeze.15) | copy-start | bytes 3145732
  24.8 2.4 %copy-start.3 = (s32[8,8]{1,0:T(8,128)S(1)}, s32[8,8]{1,0:T(8,128)}, u32[]{:S(2)}) copy-start(s32[8,8]{1,0:T(8,128)} %param.29) | copy-start | bytes 772
  26.6 2.1 %copy-start.1 = (s32[16]{0:T(128)S(1)}, s32[16]{0:T(128)}, u32[]{:S(2)}) copy-start(s32[16]{0:T(128)} %param.23) | copy-start | bytes 196
  30.2 8.0 %copy-start.5 = (f32[4096]{0:T(1024)S(1)}, f32[4096]{0:T(1024)}, u32[]{:S(2)}) copy-start(f32[4096]{0:T(1024)} %param.24) | copy-start | bytes 49156
  61.7 2.3 %collective-permute-start = (bf16[16,4,4096]{2,1,0:T(4,128)(2,1)}, bf16[16,4,4096]{2,1,0:T(4,128)(2,1)}, u32[]{:S(2)}, u32[]{:S(2)}) collective-permute-start(bf16[16,4,4096]{2,1,0:T(4,128)(2,1)} %all_to_all.15), channel_id=1, source_target_pairs={{0,1},{1,0},{2,3},{3,2},{4,5},{5,4},{6,7},{7,6},{8,9},{9,8},{10,11... | collective-permute-start | bytes 1572872 | tf_op jit(solution)/shard_map/ppermute | solution.py:23
  77.2 3.0 %collective-permute-start.1 = (f32[16,4,4096]{2,1,0:T(4,128)}, f32[16,4,4096]{2,1,0:T(4,128)}, u32[]{:S(2)}, u32[]{:S(2)}) collective-permute-start(f32[16,4,4096]{2,1,0:T(4,128)} %slice_select_fusion), channel_id=1, source_target_pairs={{0,1},{1,0},{2,3},{3,2},{4,5},{5,4},{6,7},{7,6},{8,9},{9,8},{10,11... | collective-permute-start | bytes 3145736 | tf_op jit(solution)/shard_map/ppermute | solution.py:23
  77.4 10.8 %copy-start.9 = (bf16[4096,8]{0,1:T(8,128)(2,1)S(1)}, bf16[4096,8]{0,1:T(8,128)(2,1)}, u32[]{:S(2)}) copy-start(bf16[4096,8]{0,1:T(8,128)(2,1)} %param.25) | copy-start | bytes 196612
  83.9 18.6 %all-to-all-start.2 = ((bf16[16,4,4096]{2,1,0:T(4,128)(2,1)}), bf16[16,4,4096]{2,1,0:T(4,128)(2,1)}, u32[]{:S(2)}, u32[]{:S(2)}) async-start(bf16[16,4,4096]{2,1,0:T(4,128)(2,1)} %add_convert_fusion), calls=%async_computation.2 | async-start | bytes 1048576 | tf_op jit(solution)/shard_map/all_to_all | solution.py:180
where the time goes:
time: 111 us; the launch traced here: 110 us
  local copies, waits for them, and re-layouts  26.4 us (24%)
  blocking collectives  20.3 us (18%)
  waiting for transfers between devices  18.4 us (17%)
  other arithmetic  16.7 us (15%)
  matrix products  15.7 us (14%)
  starting transfers between devices  12 us (11%)
    all_to_all x1, blocking collectives, local(): lax.all_to_all(outgoing_half, 'expert', split_axis=0, concat_axis=0, tile...  20.3 us
    all_to_all x1, waiting for transfers between devices, local(): lax.all_to_all(finished, 'expert', split_axis=0, concat_axis=0, tiled=True)  13.5 us
    all_to_all x1, starting transfers between devices, local(): lax.all_to_all(outgoing, 'expert', split_axis=1, concat_axis=1, tiled=True)  7.46 us
    dot_general x1, matrix products, local(): jnp.dot(activated, w_down[0], preferred_element_type=jnp.float32)  5.82 us
    ppermute x2, waiting for transfers between devices, partner(): lax.ppermute(x, axis, [(i, i ^ 1 << apart) for i in range(lax.axis_size(a...  4.88 us
    all_to_all x1, starting transfers between devices, local(): lax.all_to_all(finished, 'expert', split_axis=0, concat_axis=0, tiled=True)  4.25 us
    dot_general x1, matrix products, local(): jnp.dot(flattened, w_gate[0], preferred_element_type=jnp.float32)  3.83 us
    convert_element_type x1, other arithmetic, local(): finished = (kept + partner_part).astype(jnp.bfloat16)  3.76 us
  transfers between devices with their start and end apart: 4, of which 3 were waited for; matrix products, arithmetic and copies ran while one was open for 15% of the time, Pallas kernels for 0%

commit v1 on v0

--- a/solution.py
+++ b/solution.py
@@ -61,6 +61,33 @@
         ..., None
     ] * token_own_value.reshape(decode_tokens, KEY_VALUE_HEADS, 1, HEAD_SIZE).astype(jnp.float32)
     return blended_noise.reshape(decode_tokens, QUERY_HEADS * HEAD_SIZE).astype(jnp.bfloat16)
+
+
+def all_tokens(resid_wide, normed, spread, w_gate, w_up, w_down):
+    devices = lax.axis_size("expert")
+    seq_dev, experts = spread.shape
+    expert = lax.axis_index("expert") // 2
+    bits = devices.bit_length() - 1
+    coarse = lax.reduce_precision(spread, 8, 7)
+    fine = spread - coarse
+    pad = -2 * experts % 128
+    tail = jnp.pad(jnp.concatenate([coarse, fine], 1), ((0, 0), (0, pad))).astype(jnp.bfloat16)
+    rows = jnp.concatenate([normed, tail], 1)
+    for bit in reversed(range(bits)):
+        rows = jnp.concatenate([rows, partner(rows, "expert", bit)], 0)
+    gates = rows[:, D : D + 2 * experts].astype(jnp.float32).reshape(-1, 2, experts)
+    own = jnp.arange(experts, dtype=jnp.int32) == expert
+    gate = jnp.sum(jnp.where(own, gates, 0.0), (1, 2))
+    tokens = rows[:, :D]
+    gate_proj = jnp.dot(tokens, w_gate, preferred_element_type=jnp.float32)
+    up_proj = jnp.dot(tokens, w_up, preferred_element_type=jnp.float32)
+    activated = (jax.nn.silu(gate_proj) * up_proj).astype(jnp.bfloat16)
+    mixed = jnp.dot(activated, w_down, preferred_element_type=jnp.float32) * gate[:, None]
+    for bit in range(bits):
+        half = mixed.shape[0] // 2
+        moved = partner(mixed[half:].astype(jnp.bfloat16), "expert", bit)
+        mixed = mixed[:half] + moved.astype(jnp.float32)
+    return (resid_wide + mixed).astype(jnp.bfloat16)
 
 
 def local(
@@ -145,6 +172,9 @@
     expert_onehot = route_ids[:, :, None] == jnp.arange(experts, dtype=jnp.int32)[None, None, :]
     selected = jnp.sum(jnp.where(expert_onehot, logits[:, None, :], 0.0), -1)
     gate_weights = jax.nn.softmax(selected, -1)
+    if capacity >= seq_dev and devices & (devices - 1) == 0:
+        spread = jnp.sum(jnp.where(expert_onehot, gate_weights[:, :, None], 0.0), 1)
+        return all_tokens(resid_wide, normed, spread, w_gate[0], w_up[0], w_down[0])
     assigned = seq_dev * TOPK
     expert_ids = route_ids.reshape(assigned)
     chosen = (expert_ids[:, None] == jnp.arange(experts, dtype=jnp.int32)[None, :]).astype(

time: 111 us -> 99.1 us (0.89)
  blocking collectives: 20.3 us -> 0 us
  starting transfers between devices: 12 us -> 21 us
  waiting for transfers between devices: 18.4 us -> 26.4 us
  matrix products: 15.7 us -> 12.4 us
  local copies, waits for them, and re-layouts: 26.4 us -> 23.2 us
  other arithmetic: 16.7 us -> 14.7 us
    ppermute x2 -> x8, waiting for transfers between devices: 4.88 us -> 26.4 us  [partner(): lax.ppermute(x, axis, [(i, i ^ 1 << apart) for i in range(lax.axis_size(a...]
    all_to_all x1 -> x0, blocking collectives: 20.3 us -> none  [local(): lax.all_to_all(outgoing_half, 'expert', split_axis=0, concat_axis=0, tile...]
    all_to_all x1 -> x0, waiting for transfers between devices: 13.5 us -> none  [local(): lax.all_to_all(finished, 'expert', split_axis=0, concat_axis=0, tiled=True)]
    ppermute x2 -> x8, starting transfers between devices: 0.29 us -> 13.6 us  [partner(): lax.ppermute(x, axis, [(i, i ^ 1 << apart) for i in range(lax.axis_size(a...]
    all_to_all x1 -> x0, starting transfers between devices: 4.25 us -> none  [local(): lax.all_to_all(finished, 'expert', split_axis=0, concat_axis=0, tiled=True)]
    reshape x3 -> x0, local copies, waits for them, and re-layouts: 4.08 us -> none  [the longest x1 2.02 us: local(): outgoing_half = gathered_rows.reshape(devices, half_cap, D)]
    dot_general x3 -> x2, matrix products: 10.8 us -> 6.92 us  [the longest x1 4.98 us: all_tokens(): jnp.dot(activated, w_down, preferred_element_type=jnp.float32)]
    convert_element_type x3 -> x2, other arithmetic: 4.48 us -> 0.74 us  [the longest x1 0.66 us: all_tokens(): return (resid_wide + mixed).astype(jnp.bfloat16)]
  transfers between devices with their start and end apart: 4 -> 9, of which waited for: 3 -> 8; matrix products, arithmetic and copies ran while one was open for 15% -> 20% of each run, Pallas kernels for 0% -> 0%
where the time goes in v1:
time: 99.1 us; the launch traced here: 98.2 us
  waiting for transfers between devices  26.4 us (27%)
  local copies, waits for them, and re-layouts  23.2 us (23%)
  starting transfers between devices  21 us (21%)
  other arithmetic  14.7 us (15%)
  matrix products  12.4 us (13%)
    ppermute x8, waiting for transfers between devices, partner(): lax.ppermute(x, axis, [(i, i ^ 1 << apart) for i in range(lax.axis_size(a...  26.4 us
    ppermute x8, starting transfers between devices, partner(): lax.ppermute(x, axis, [(i, i ^ 1 << apart) for i in range(lax.axis_size(a...  13.6 us
    all_to_all x1, starting transfers between devices, local(): lax.all_to_all(outgoing, 'expert', split_axis=1, concat_axis=1, tiled=True)  7.46 us
    unnamed x36, local copies, waits for them, and re-layouts  5.18 us
    dot_general x1, matrix products, all_tokens(): jnp.dot(activated, w_down, preferred_element_type=jnp.float32)  4.98 us
    gather x1, local copies, waits for them, and re-layouts, local(): fetched = local_kv[page_table]  3.07 us
    dot_general x2, matrix products, attend(): jnp.einsum('tkgd,tlkd->tkgl', heads_of_queries, heads_of_keys, preferred_...  3.04 us
    another operation x2, local copies, waits for them, and re-layouts, attend(): rows_of_keys.reshape(decode_tokens, -1, KEY_VALUE_HEADS, HEAD_SIZE)  3 us
  transfers between devices with their start and end apart: 9, of which 8 were waited for; matrix products, arithmetic and copies ran while one was open for 20% of the time, Pallas kernels for 0%

profile of v1, /device:TPU:0, one launch (start us, length us, event | category | flops | bytes accessed | tf_op | source)
XLA Modules:
  0.0 98.2 jit_solution(18162269884148207099)
XLA Ops:
  2.8 2.3 %gather_fusion.1 = bf16[32,2,16,256]{3,2,1,0:T(8,128)(2,1)} fusion(bf16[16,2,16,256]{3,2,1,0:T(8,128)(2,1)} %bitcast.87, s32[1024]{0:T(1024)S(1)} %get-tuple-element.26), kind=kCustom, calls=%fused_computation.1 | custom fusion | bytes 1048704 | tf_op jit(solution)/shard_map/jit(_take)/gather | solution.py:131
  7.2 7.5 %all-to-all-start = ((bf16[2,16,2,16,256]{4,3,0,2,1:T(8,128)(2,1)}), bf16[2,16,2,16,256]{4,3,0,2,1:T(8,128)(2,1)}, u32[]{:S(2)}, u32[]{:S(2)}) async-start(bf16[2,16,2,16,256]{4,3,0,2,1:T(8,128)(2,1)} %copy.48), calls=%async_computation | async-start | bytes 1048576 | tf_op jit(solution)/shard_map/all_to_all | solution.py:135
  14.7 3.1 %gather_fusion.2 = bf16[128,2,16,256]{3,2,1,0:T(8,128)(2,1)} fusion(bf16[32,2,16,256]{3,2,1,0:T(8,128)(2,1)} %param.18, s32[1024]{0:T(1024)S(1)} %get-tuple-element.25), kind=kCustom, calls=%fused_computation.2 | custom fusion | bytes 4194816 | tf_op jit(solution)/shard_map/gather | solution.py:150
  17.8 3.0 %slice_bitcast_fusion.1 = (bf16[8,16,1,16,256]{4,3,1,0,2:T(8,128)(2,1)}, bf16[8,16,1,16,256]{4,3,1,0,2:T(8,128)(2,1)}) fusion(bf16[8,16,2,16,256]{4,3,2,1,0:T(8,128)(2,1)} %bitcast.85), kind=kLoop, calls=%fused_computation.22 | loop fusion | bytes 4194304
  20.8 2.2 %reshape_reshape_squeeze.15 = bf16[8,256,2,128]{3,2,1,0:T(2,128)(2,1)} reshape(bf16[8,16,1,16,256]{4,3,1,0,2:T(8,128)(2,1)} %get-tuple-element.8) | data formatting | bytes 2097152 | tf_op jit(solution)/shard_map/reshape;reshape;squeeze | solution.py:32
  23.0 2.2 %reshape_reshape_squeeze.14 = bf16[8,256,2,128]{3,2,1,0:T(2,128)(2,1)} reshape(bf16[8,16,1,16,256]{4,3,1,0,2:T(8,128)(2,1)} %get-tuple-element.7) | data formatting | bytes 2097152 | tf_op jit(solution)/shard_map/reshape;reshape;squeeze | solution.py:31
  25.5 1.8 %fusion.66 = (f32[8,2,16]{2,1,0:T(2,128)S(1)}, f32[8,2,16,256]{3,2,1,0:T(8,128)S(1)}) fusion(bf16[8,2,16,128]{3,0,2,1:T(8,128)(2,1)S(1)} %bitcast.103, bf16[8,256,2,128]{3,2,1,0:T(2,128)(2,1)} %reshape_reshape_squeeze.14, pred[8,256]{1,0:T(8,128)(4,1)S(1)} %broadcast_compare_fusion), kind=kOutput, calls=%fused_computation.142 | convolution fusion | flops 16973568 | bytes 1379328 | tf_op jit(solution)/shard_map/tkgd,tlkd->tkgl/dot_general | solution.py:36
  32.4 1.8 %fusion.65 = (bf16[2,16,1,16,256]{4,3,0,2,1:T(8,128)(2,1)}, bf16[2,16,1,16,256]{4,3,0,2,1:T(8,128)(2,1)S(1)}) fusion(bf16[2,16,2,16,256]{4,3,0,2,1:T(8,128)(2,1)} %all-to-all-done), kind=kLoop, calls=%fused_computation.141 | loop fusion | bytes 1048576 | tf_op jit(solution)/shard_map/slice | solution.py:137
  43.9 2.8 %collective-permute-start = (bf16[8,4224]{1,0:T(8,128)(2,1)S(1)}, bf16[8,4224]{1,0:T(8,128)(2,1)S(1)}, u32[]{:S(2)}, u32[]{:S(2)}) collective-permute-start(bf16[8,4224]{1,0:T(8,128)(2,1)S(1)} %get-tuple-element.11), channel_id=1, source_target_pairs={{0,8},{1,9},{2,10},{3,11},{4,12},{5,13},{6,14},{7,15},{8,0},{9,1},... | collective-permute-start | bytes 202760 | tf_op jit(solution)/shard_map/ppermute | solution.py:23
  46.8 3.9 %collective-permute-done = bf16[8,4224]{1,0:T(8,128)(2,1)S(1)} collective-permute-done((bf16[8,4224]{1,0:T(8,128)(2,1)S(1)}, bf16[8,4224]{1,0:T(8,128)(2,1)S(1)}, u32[]{:S(2)}, u32[]{:S(2)}) %collective-permute-start) | collective-permute-done | bytes 67616 | tf_op jit(solution)/shard_map/ppermute | solution.py:23
  52.0 3.8 %collective-permute-done.1 = bf16[16,4224]{1,0:T(8,128)(2,1)S(1)} collective-permute-done((bf16[16,4224]{1,0:T(8,128)(2,1)S(1)}, bf16[16,4224]{1,0:T(8,128)(2,1)S(1)}, u32[]{:S(2)}, u32[]{:S(2)}) %collective-permute-start.1) | collective-permute-done | bytes 135200 | tf_op jit(solution)/shard_map/ppermute | solution.py:23
  55.8 1.8 %collective-permute-start.2 = (bf16[32,4224]{1,0:T(8,128)(2,1)S(1)}, bf16[32,4224]{1,0:T(8,128)(2,1)S(1)}, u32[]{:S(2)}, u32[]{:S(2)}) collective-permute-start(bf16[32,4224]{1,0:T(8,128)(2,1)S(1)} %pad_maximum_fusion.1), channel_id=1, source_target_pairs={{0,2},{1,3},{2,0},{3,1},{4,6},{5,7},{6,4},{7,5},{8,10},{9,11},{10,... | collective-permute-start | bytes 811016 | tf_op jit(solution)/shard_map/ppermute | solution.py:23
  58.3 4.0 %collective-permute-done.2 = bf16[32,4224]{1,0:T(8,128)(2,1)S(1)} collective-permute-done((bf16[32,4224]{1,0:T(8,128)(2,1)S(1)}, bf16[32,4224]{1,0:T(8,128)(2,1)S(1)}, u32[]{:S(2)}, u32[]{:S(2)}) %collective-permute-start.2) | collective-permute-done | bytes 270368 | tf_op jit(solution)/shard_map/ppermute | solution.py:23
  66.1 1.9 %fusion.1 = f32[128,384]{1,0:T(8,128)S(1)} fusion(bf16[1,4096,384]{2,1,0:T(8,128)(2,1)S(1)} %copy-done.2, bf16[128,4224]{1,0:T(8,128)(2,1)} %constant_dynamic-update-slice_fusion), kind=kOutput, calls=%fused_computation.5 | convolution fusion | flops 402653184 | bytes 4390912 | tf_op jit(solution)/shard_map/dot_general | solution.py:83
  68.0 5.0 %convolution_multiply_fusion = f32[128,4096]{1,0:T(8,128)} fusion(bf16[1,384,4096]{2,1,0:T(8,128)(2,1)S(1)} %copy-done, f32[128]{0:T(128)S(1)} %select_reduce_fusion, f32[128,384]{1,0:T(8,128)S(1)} %fusion.1, bf16[1,4096,384]{2,1,0:T(8,128)(2,1)} %param.26, bf16[128,4224]{1,0:T(8,128)(2,1)} %constant_dynamic-update-slice_fusion), kind=kOutput, calls=%fused_computation.3 | convolution fusion | flops 806125568 | bytes 9634304 | tf_op jit(solution)/shard_map/dot_general | solution.py:85
  73.0 1.3 %slice.146 = bf16[64,4096]{1,0:T(8,128)(2,1)S(1)} slice(f32[128,4096]{1,0:T(8,128)} %convolution_multiply_fusion), slice={[64:128], [0:4096]} | slice | bytes 1048576 | tf_op jit(solution)/shard_map/slice | solution.py:88
  74.5 1.8 %collective-permute-done.4 = bf16[64,4096]{1,0:T(8,128)(2,1)S(1)} collective-permute-done((bf16[64,4096]{1,0:T(8,128)(2,1)S(1)}, bf16[64,4096]{1,0:T(8,128)(2,1)S(1)}, u32[]{:S(2)}, u32[]{:S(2)}) %collective-permute-start.4) | collective-permute-done | bytes 524320 | tf_op jit(solution)/shard_map/ppermute | solution.py:23
  76.3 1.3 %slice_add_fusion = f32[64,4096]{1,0:T(8,128)S(1)} fusion(f32[128,4096]{1,0:T(8,128)} %convolution_multiply_fusion, bf16[64,4096]{1,0:T(8,128)(2,1)S(1)} %collective-permute-done.4), kind=kLoop, calls=%fused_computation.20 | loop fusion | flops 524288 | bytes 2621440 | tf_op jit(solution)/shard_map/add | solution.py:89
  77.6 1.8 %collective-permute-start.5 = (bf16[32,4096]{1,0:T(8,128)(2,1)S(1)}, bf16[32,4096]{1,0:T(8,128)(2,1)S(1)}, u32[]{:S(2)}, u32[]{:S(2)}) collective-permute-start(bf16[32,4096]{1,0:T(8,128)(2,1)S(1)} %slice.147), channel_id=1, source_target_pairs={{0,2},{1,3},{2,0},{3,1},{4,6},{5,7},{6,4},{7,5},{8,10},{9,11},{10,... | collective-permute-start | bytes 786440 | tf_op jit(solution)/shard_map/ppermute | solution.py:23
  79.4 6.6 %collective-permute-done.5 = bf16[32,4096]{1,0:T(8,128)(2,1)S(1)} collective-permute-done((bf16[32,4096]{1,0:T(8,128)(2,1)S(1)}, bf16[32,4096]{1,0:T(8,128)(2,1)S(1)}, u32[]{:S(2)}, u32[]{:S(2)}) %collective-permute-start.5) | collective-permute-done | bytes 262176 | tf_op jit(solution)/shard_map/ppermute | solution.py:23
  86.1 2.2 %collective-permute-start.6 = (bf16[16,4096]{1,0:T(8,128)(2,1)S(1)}, bf16[16,4096]{1,0:T(8,128)(2,1)S(1)}, u32[]{:S(2)}, u32[]{:S(2)}) collective-permute-start(bf16[16,4096]{1,0:T(8,128)(2,1)S(1)} %slice.148), channel_id=1, source_target_pairs={{0,4},{1,5},{2,6},{3,7},{4,0},{5,1},{6,2},{7,3},{8,12},{9,13},{10,... | collective-permute-start | bytes 393224 | tf_op jit(solution)/shard_map/ppermute | solution.py:23
  88.3 2.9 %collective-permute-done.6 = bf16[16,4096]{1,0:T(8,128)(2,1)S(1)} collective-permute-done((bf16[16,4096]{1,0:T(8,128)(2,1)S(1)}, bf16[16,4096]{1,0:T(8,128)(2,1)S(1)}, u32[]{:S(2)}, u32[]{:S(2)}) %collective-permute-start.6) | collective-permute-done | bytes 131104 | tf_op jit(solution)/shard_map/ppermute | solution.py:23
  91.3 4.0 %collective-permute-start.7 = (bf16[8,4096]{1,0:T(8,128)(2,1)S(1)}, bf16[8,4096]{1,0:T(8,128)(2,1)S(1)}, u32[]{:S(2)}, u32[]{:S(2)}) collective-permute-start(bf16[8,4096]{1,0:T(8,128)(2,1)S(1)} %slice.149), channel_id=1, source_target_pairs={{0,8},{1,9},{2,10},{3,11},{4,12},{5,13},{6,14},{7,15},{8,0},{9,1},... | collective-permute-start | bytes 196616 | tf_op jit(solution)/shard_map/ppermute | solution.py:23
  95.3 2.2 %collective-permute-done.7 = bf16[8,4096]{1,0:T(8,128)(2,1)S(1)} collective-permute-done((bf16[8,4096]{1,0:T(8,128)(2,1)S(1)}, bf16[8,4096]{1,0:T(8,128)(2,1)S(1)}, u32[]{:S(2)}, u32[]{:S(2)}) %collective-permute-start.7) | collective-permute-done | bytes 65568 | tf_op jit(solution)/shard_map/ppermute | solution.py:23
  (109 shorter events, 26.7 us)
Async XLA Ops:
  0.0 68.0 %copy-start = (bf16[1,384,4096]{2,1,0:T(8,128)(2,1)S(1)}, bf16[1,384,4096]{2,1,0:T(8,128)(2,1)}, u32[]{:S(2)}) copy-start(bf16[1,384,4096]{2,1,0:T(8,128)(2,1)} %param.28) | copy-start | bytes 9437188
  7.2 25.2 %all-to-all-start = ((bf16[2,16,2,16,256]{4,3,0,2,1:T(8,128)(2,1)}), bf16[2,16,2,16,256]{4,3,0,2,1:T(8,128)(2,1)}, u32[]{:S(2)}, u32[]{:S(2)}) async-start(bf16[2,16,2,16,256]{4,3,0,2,1:T(8,128)(2,1)} %copy.48), calls=%async_computation | async-start | bytes 1048576 | tf_op jit(solution)/shard_map/all_to_all | solution.py:135
  23.0 2.2 %copy-start.7 = (bf16[8,2,256]{2,1,0:T(2,128)(2,1)S(1)}, bf16[8,2,256]{2,1,0:T(2,128)(2,1)}, u32[]{:S(2)}) copy-start(bf16[8,2,256]{2,1,0:T(2,128)(2,1)} %param.17) | copy-start | bytes 24580
  23.0 2.3 %copy-start.13 = (s32[8]{0:T(128)S(1)}, s32[8]{0:T(128)}, u32[]{:S(2)}) copy-start(s32[8]{0:T(128)} %param.20) | copy-start | bytes 100
  23.0 2.4 %copy-start.11 = (bf16[8,4096]{1,0:T(8,128)(2,1)S(1)}, bf16[8,4096]{1,0:T(8,128)(2,1)}, u32[]{:S(2)}) copy-start(bf16[8,4096]{1,0:T(8,128)(2,1)} %param.16) | copy-start | bytes 196612
  25.5 2.1 %copy-start.3 = (bf16[8,256,2,128]{3,2,1,0:T(2,128)(2,1)S(1)}, bf16[8,256,2,128]{3,2,1,0:T(2,128)(2,1)}, u32[]{:S(2)}) copy-start(bf16[8,256,2,128]{3,2,1,0:T(2,128)(2,1)} %reshape_reshape_squeeze.15) | copy-start | bytes 3145732
  27.5 1.2 %copy-start.1 = (s32[16]{0:T(128)S(1)}, s32[16]{0:T(128)}, u32[]{:S(2)}) copy-start(s32[16]{0:T(128)} %param.23) | copy-start | bytes 196
  27.9 6.3 %copy-start.4 = (bf16[8,2,16,128]{3,2,1,0:T(8,128)(2,1)}, bf16[8,2,16,128]{3,2,1,0:T(8,128)(2,1)S(1)}, u32[]{:S(2)}) copy-start(bf16[8,2,16,128]{3,2,1,0:T(8,128)(2,1)S(1)} %fusion.7) | copy-start | bytes 196612
  28.7 5.4 %copy-start.10 = (bf16[1,2,32,128]{3,2,1,0:T(8,128)(2,1)}, bf16[1,2,32,128]{3,2,1,0:T(8,128)(2,1)S(1)}, u32[]{:S(2)}) copy-start(bf16[1,2,32,128]{3,2,1,0:T(8,128)(2,1)S(1)} %copy.66) | copy-start | bytes 49156
  34.9 6.4 %slice-start = ((bf16[8,2,16,128]{3,2,1,0:T(8,128)(2,1)}), bf16[2,2,16,128]{3,2,1,0:T(8,128)(2,1)S(1)}, s32[]{:S(2)}) async-start(bf16[8,2,16,128]{3,2,1,0:T(8,128)(2,1)} %copy-done.4), calls=%async_computation.1 | async-start | bytes 32768 | tf_op jit(solution)/shard_map/slice | solution.py:162
  34.9 6.5 %copy-start.5 = (bf16[8,4096]{1,0:T(8,128)(2,1)S(1)}, bf16[8,4096]{1,0:T(8,128)(2,1)}, u32[]{:S(2)}) copy-start(bf16[8,4096]{1,0:T(8,128)(2,1)} %param.15) | copy-start | bytes 196612
  36.7 4.6 %copy-start.12 = (pred[2]{0:T(512)(128)(4,1)S(1)}, pred[2]{0:T(512)(128)(4,1)}, u32[]{:S(2)}) copy-start(pred[2]{0:T(512)(128)(4,1)} %iota_compare_fusion.6) | copy-start | bytes 10
  36.7 4.9 %copy-start.8 = (f32[4096]{0:T(1024)S(1)}, f32[4096]{0:T(1024)}, u32[]{:S(2)}) copy-start(f32[4096]{0:T(1024)} %param.24) | copy-start | bytes 49156
  36.7 5.0 %copy-start.6 = (bf16[4096,8]{0,1:T(8,128)(2,1)S(1)}, bf16[4096,8]{0,1:T(8,128)(2,1)}, u32[]{:S(2)}) copy-start(bf16[4096,8]{0,1:T(8,128)(2,1)} %param.25) | copy-start | bytes 196612
  36.7 5.2 %copy-start.9 = (s32[8,8]{1,0:T(8,128)S(1)}, s32[8,8]{1,0:T(8,128)}, u32[]{:S(2)}) copy-start(s32[8,8]{1,0:T(8,128)} %param.29) | copy-start | bytes 772
  43.9 6.7 %collective-permute-start = (bf16[8,4224]{1,0:T(8,128)(2,1)S(1)}, bf16[8,4224]{1,0:T(8,128)(2,1)S(1)}, u32[]{:S(2)}, u32[]{:S(2)}) collective-permute-start(bf16[8,4224]{1,0:T(8,128)(2,1)S(1)} %get-tuple-element.11), channel_id=1, source_target_pairs={{0,8},{1,9},{2,10},{3,11},{4,12},{5,13},{6,14},{7,15},{8,0},{9,1},... | collective-permute-start | bytes 202760 | tf_op jit(solution)/shard_map/ppermute | solution.py:23
  50.7 5.1 %collective-permute-start.1 = (bf16[16,4224]{1,0:T(8,128)(2,1)S(1)}, bf16[16,4224]{1,0:T(8,128)(2,1)S(1)}, u32[]{:S(2)}, u32[]{:S(2)}) collective-permute-start(bf16[16,4224]{1,0:T(8,128)(2,1)S(1)} %pad_maximum_fusion.2), channel_id=1, source_target_pairs={{0,4},{1,5},{2,6},{3,7},{4,0},{5,1},{6,2},{7,3},{8,12},{9,13},{10,... | collective-permute-start | bytes 405512 | tf_op jit(solution)/shard_map/ppermute | solution.py:23
  55.8 10.3 %copy-start.2 = (bf16[1,4096,384]{2,1,0:T(8,128)(2,1)S(1)}, bf16[1,4096,384]{2,1,0:T(8,128)(2,1)}, u32[]{:S(2)}) copy-start(bf16[1,4096,384]{2,1,0:T(8,128)(2,1)} %param.27) | copy-start | bytes 9437188
  55.8 6.5 %collective-permute-start.2 = (bf16[32,4224]{1,0:T(8,128)(2,1)S(1)}, bf16[32,4224]{1,0:T(8,128)(2,1)S(1)}, u32[]{:S(2)}, u32[]{:S(2)}) collective-permute-start(bf16[32,4224]{1,0:T(8,128)(2,1)S(1)} %pad_maximum_fusion.1), channel_id=1, source_target_pairs={{0,2},{1,3},{2,0},{3,1},{4,6},{5,7},{6,4},{7,5},{8,10},{9,11},{10,... | collective-permute-start | bytes 811016 | tf_op jit(solution)/shard_map/ppermute | solution.py:23
  62.4 2.0 %collective-permute-start.3 = (bf16[64,4224]{1,0:T(8,128)(2,1)S(1)}, bf16[64,4224]{1,0:T(8,128)(2,1)S(1)}, u32[]{:S(2)}, u32[]{:S(2)}) collective-permute-start(bf16[64,4224]{1,0:T(8,128)(2,1)S(1)} %pad_maximum_fusion), channel_id=1, source_target_pairs={{0,1},{1,0},{2,3},{3,2},{4,5},{5,4},{6,7},{7,6},{8,9},{9,8},{10,11... | collective-permute-start | bytes 1622024 | tf_op jit(solution)/shard_map/ppermute | solution.py:23
  74.3 2.0 %collective-permute-start.4 = (bf16[64,4096]{1,0:T(8,128)(2,1)S(1)}, bf16[64,4096]{1,0:T(8,128)(2,1)S(1)}, u32[]{:S(2)}, u32[]{:S(2)}) collective-permute-start(bf16[64,4096]{1,0:T(8,128)(2,1)S(1)} %slice.146), channel_id=1, source_target_pairs={{0,1},{1,0},{2,3},{3,2},{4,5},{5,4},{6,7},{7,6},{8,9},{9,8},{10,11... | collective-permute-start | bytes 1572872 | tf_op jit(solution)/shard_map/ppermute | solution.py:23
  77.6 8.4 %collective-permute-start.5 = (bf16[32,4096]{1,0:T(8,128)(2,1)S(1)}, bf16[32,4096]{1,0:T(8,128)(2,1)S(1)}, u32[]{:S(2)}, u32[]{:S(2)}) collective-permute-start(bf16[32,4096]{1,0:T(8,128)(2,1)S(1)} %slice.147), channel_id=1, source_target_pairs={{0,2},{1,3},{2,0},{3,1},{4,6},{5,7},{6,4},{7,5},{8,10},{9,11},{10,... | collective-permute-start | bytes 786440 | tf_op jit(solution)/shard_map/ppermute | solution.py:23
  86.1 5.1 %collective-permute-start.6 = (bf16[16,4096]{1,0:T(8,128)(2,1)S(1)}, bf16[16,4096]{1,0:T(8,128)(2,1)S(1)}, u32[]{:S(2)}, u32[]{:S(2)}) collective-permute-start(bf16[16,4096]{1,0:T(8,128)(2,1)S(1)} %slice.148), channel_id=1, source_target_pairs={{0,4},{1,5},{2,6},{3,7},{4,0},{5,1},{6,2},{7,3},{8,12},{9,13},{10,... | collective-permute-start | bytes 393224 | tf_op jit(solution)/shard_map/ppermute | solution.py:23
  91.3 6.2 %collective-permute-start.7 = (bf16[8,4096]{1,0:T(8,128)(2,1)S(1)}, bf16[8,4096]{1,0:T(8,128)(2,1)S(1)}, u32[]{:S(2)}, u32[]{:S(2)}) collective-permute-start(bf16[8,4096]{1,0:T(8,128)(2,1)S(1)} %slice.149), channel_id=1, source_target_pairs={{0,8},{1,9},{2,10},{3,11},{4,12},{5,13},{6,14},{7,15},{8,0},{9,1},... | collective-permute-start | bytes 196616 | tf_op jit(solution)/shard_map/ppermute | solution.py:23

commit v2 on v0

v2 whole, which is shorter than its diff:
```python
import functools
import math

import jax
import jax.numpy as jnp
from jax import lax
from jax.experimental import pallas as pl
from jax.experimental.pallas import tpu as pltpu
from jax.sharding import PartitionSpec as P

D = 4096
QUERY_HEADS = 32
KEY_VALUE_HEADS = 2
HEAD_SIZE = 128
PAGE_TOKENS = 16
TOPK = 8
MAXB = 16
MAXP = 2


norm_eps = 1e-06
masked_score = -1e30


def partner(x, axis, apart):
    return lax.ppermute(x, axis, [(i, i ^ 1 << apart) for i in range(lax.axis_size(axis))])


def swap(x, axis, offset):
    return lax.ppermute(x, axis, [(i, i ^ offset) for i in range(lax.axis_size(axis))])


def whole(space):
    return pl.BlockSpec(memory_space=space)


VM, SM = whole(pltpu.VMEM), whole(pltpu.SMEM)
MIB = 1 << 20


def pack_kernel(owner, pages, out, source, count):
    def clear(i, _):
        source[i] = 0
        return 0

    def clear_count(i, _):
        count[i] = 0
        return 0

    def place(p, _):
        o = owner[p]
        r = count[o]
        source[o * MAXP + r] = p
        count[o] = r + 1
        return 0

    def move(i, _):
        out[i] = pages[source[i]]
        return 0

    lax.fori_loop(0, source.shape[0], clear, 0, unroll=8)
    lax.fori_loop(0, count.shape[0], clear_count, 0, unroll=8)
    lax.fori_loop(0, owner.shape[0], place, 0, unroll=8)
    lax.fori_loop(0, out.shape[0], move, 0, unroll=8)


def pack(prompt_owner, pages, devices):
    return pl.pallas_call(
        pack_kernel,
        out_shape=jax.ShapeDtypeStruct((devices * MAXP,) + pages.shape[1:], pages.dtype),
        in_specs=[SM, VM],
        out_specs=VM,
        scratch_shapes=[pltpu.SMEM((devices * MAXP,), jnp.int32), pltpu.SMEM((devices,), jnp.int32)],
        compiler_params=pltpu.CompilerParams(vmem_limit_bytes=16 * MIB),
        name="pack_pages",
    )(prompt_owner, pages)


def pool_attention(wide, keys, values, counts, own_key, own_value):
    group, seqs, size = wide.shape
    scale = 1.0 / math.sqrt(HEAD_SIZE)
    flat = wide.reshape(group * seqs, size).astype(jnp.bfloat16)
    scores = (
        lax.dot_general(flat, keys, (((1,), (1,)), ((), ())), preferred_element_type=jnp.float32)
        * scale
    ).reshape(group, seqs, keys.shape[0])
    allowed = (counts > 0.0)[None]
    scores = jnp.where(allowed, scores, masked_score)
    own_score = jnp.sum(wide * own_key[None], -1, keepdims=True) * scale
    peak = jnp.maximum(jnp.max(scores, -1, keepdims=True), own_score)
    weights = jnp.where(allowed, jnp.exp(scores - peak), 0.0) * counts[None]
    own_weight = jnp.exp(own_score - peak)
    inverse = 1.0 / (jnp.sum(weights, -1, keepdims=True) + own_weight)
    probs = (weights * inverse).astype(jnp.bfloat16).reshape(group * seqs, keys.shape[0])
    own_prob = (own_weight * inverse).astype(jnp.bfloat16).astype(jnp.float32)
    out = jnp.dot(probs, values, preferred_element_type=jnp.float32).reshape(group, seqs, size)
    return out + own_prob * own_value[None]


def head_slabs(queries, g):
    group = QUERY_HEADS // KEY_VALUE_HEADS
    return jnp.concatenate(
        [
            queries[:, (g * group + j) * HEAD_SIZE : (g * group + j + 1) * HEAD_SIZE].astype(
                jnp.float32
            )[None]
            for j in range(group)
        ],
        0,
    )


def local_kernel(blocks, queries, own_kv, pool, table, out):
    seqs = queries.shape[0]
    tokens = pool.shape[0] * PAGE_TOKENS
    page = lax.broadcasted_iota(jnp.int32, (seqs, tokens), 1) // PAGE_TOKENS
    row = lax.broadcasted_iota(jnp.int32, (seqs, 1), 0)
    limit = jnp.zeros((seqs, 1), jnp.int32)
    for s in range(seqs):
        limit = jnp.where(row == s, blocks[s], limit)
    counts = jnp.zeros((seqs, tokens), jnp.float32)
    for b in range(table.shape[1]):
        entry = jnp.where(limit > b, table[:, b : b + 1], -1)
        counts = counts + jnp.where(page == entry, 1.0, 0.0)
    group = QUERY_HEADS // KEY_VALUE_HEADS
    for g in range(KEY_VALUE_HEADS):
        cols = slice(g * HEAD_SIZE, (g + 1) * HEAD_SIZE)
        result = pool_attention(
            head_slabs(queries, g),
            pool[:, 0, :, cols].reshape(tokens, HEAD_SIZE),
            pool[:, 1, :, cols].reshape(tokens, HEAD_SIZE),
            counts,
            own_kv[:, 0, cols].astype(jnp.float32),
            own_kv[:, 1, cols].astype(jnp.float32),
        )
        for j in range(group):
            at = (g * group + j) * HEAD_SIZE
            out[:, at : at + HEAD_SIZE] = result[j].astype(jnp.bfloat16)


def local_attention(seq_blocks, queries, own_kv, pool, page_table):
    return pl.pallas_call(
        local_kernel,
        out_shape=jax.ShapeDtypeStruct(queries.shape, jnp.bfloat16),
        in_specs=[SM, VM, VM, VM, VM],
        out_specs=VM,
        compiler_params=pltpu.CompilerParams(vmem_limit_bytes=16 * MIB),
        name="local_attention",
    )(seq_blocks, queries, own_kv, pool, page_table)


def head_kernel(
    tail, position, owner, lengths, queries, own_kv, arrived, old, hidden, gain, router, routes,
    residual, payload, spread, mixed,
):
    seqs = queries.shape[0]
    width = queries.shape[1]
    experts = router.shape[1]
    tokens = arrived.shape[0] * PAGE_TOKENS
    here = position[0]

    def find(p, carry):
        found = carry[0]
        mine = owner[p] == here
        picked = [
            jnp.where(mine & (found == r), lengths[p], carry[1 + r]) for r in range(MAXP)
        ]
        return (jnp.where(mine, found + 1, found), *picked)

    state = lax.fori_loop(
        0, owner.shape[0], find, (jnp.int32(0),) * (1 + MAXP), unroll=8
    )
    new_count = state[0]
    row = lax.broadcasted_iota(jnp.int32, (seqs, 1), 0)
    page = lax.broadcasted_iota(jnp.int32, (seqs, tokens), 1) // PAGE_TOKENS
    counts = jnp.concatenate(
        [
            jnp.where((page < state[1 + r]) & (row == r), 1.0, 0.0)
            for r in range(MAXP)
        ],
        1,
    )
    is_new = row < new_count
    group = QUERY_HEADS // KEY_VALUE_HEADS
    for g in range(KEY_VALUE_HEADS):
        cols = slice(g * HEAD_SIZE, (g + 1) * HEAD_SIZE)

        def side(kv):
            return jnp.concatenate(
                [arrived[:, r, kv, :, cols].reshape(tokens, HEAD_SIZE) for r in range(MAXP)], 0
            )

        result = pool_attention(
            head_slabs(queries, g),
            side(0),
            side(1),
            counts,
            own_kv[:, 0, cols].astype(jnp.float32),
            own_kv[:, 1, cols].astype(jnp.float32),
        )
        for j in range(group):
            at = slice((g * group + j) * HEAD_SIZE, (g * group + j + 1) * HEAD_SIZE)
            fresh = result[j].astype(jnp.bfloat16).astype(jnp.float32)
            chosen = jnp.where(is_new, fresh, old[:, at].astype(jnp.float32))
            mixed[:, at] = hidden[:, at].astype(jnp.float32) + chosen
    summed = mixed[...].astype(jnp.bfloat16)
    residual[...] = summed
    wide = summed.astype(jnp.float32)
    level = lax.rsqrt(jnp.mean(wide * wide, -1, keepdims=True) + norm_eps)
    normed = (wide * level * gain[...]).astype(jnp.bfloat16)
    payload[:, :width] = normed
    logits = jnp.dot(normed, router[...], preferred_element_type=jnp.float32)
    lane = lax.broadcasted_iota(jnp.int32, (seqs, experts), 1)
    chosen = jnp.zeros((seqs, experts), jnp.float32)
    for k in range(routes.shape[1]):
        chosen = chosen + jnp.where(routes[:, k : k + 1] == lane, 1.0, 0.0)
    top = jnp.max(jnp.where(chosen > 0.0, logits, masked_score), -1, keepdims=True)
    powers = jnp.where(chosen > 0.0, jnp.exp(logits - top), 0.0) * chosen
    gates = powers / jnp.sum(powers, -1, keepdims=True)
    spread[...] = gates
    if tail:
        payload[:, width:] = jnp.zeros((seqs, tail), jnp.bfloat16)
        coarse = gates.astype(jnp.bfloat16)
        payload[:, width : width + experts] = coarse
        fine = (gates - coarse.astype(jnp.float32)).astype(jnp.bfloat16)
        payload[:, width + tail // 2 : width + tail // 2 + experts] = fine


def finish_heads(
    tail, position, prompt_owner, prompt_pages, queries, own_kv, arrived, old, hidden, gain, router, routes
):
    seqs, width = queries.shape
    return pl.pallas_call(
        functools.partial(head_kernel, tail),
        out_shape=(
            jax.ShapeDtypeStruct((seqs, width), jnp.bfloat16),
            jax.ShapeDtypeStruct((seqs, width + tail), jnp.bfloat16),
            jax.ShapeDtypeStruct((seqs, router.shape[1]), jnp.float32),
        ),
        in_specs=[SM, SM, SM] + [VM] * 8,
        out_specs=(VM, VM, VM),
        scratch_shapes=[pltpu.VMEM((seqs, width), jnp.float32)],
        compiler_params=pltpu.CompilerParams(vmem_limit_bytes=32 * MIB),
        name="finish_heads",
    )(
        position, prompt_owner, prompt_pages, queries, own_kv, arrived, old, hidden, gain, router, routes
    )


def expert_kernel(
    tail, expert, near, across, core_near, core_across, w_gate, w_up, w_down,
    near_out, across_out, core_near_out, core_across_out,
):
    width = w_gate.shape[0]
    share = near.shape[0]
    blocks = (near, across, core_near, core_across)
    tokens = jnp.concatenate([block[:, :width] for block in blocks], 0)
    ends = jnp.concatenate([block[:, width:].astype(jnp.float32) for block in blocks], 0)
    lane = lax.broadcasted_iota(jnp.int32, ends.shape, 1)
    wanted = (lane == expert[0]) | (lane == expert[0] + tail // 2)
    gate = jnp.sum(jnp.where(wanted, ends, 0.0), -1, keepdims=True)
    gate_proj = jnp.dot(tokens, w_gate[...], preferred_element_type=jnp.float32)
    up_proj = jnp.dot(tokens, w_up[...], preferred_element_type=jnp.float32)
    activated = (gate_proj / (1.0 + jnp.exp(-gate_proj)) * up_proj).astype(jnp.bfloat16)
    step = min(width, 1024)
    for at in range(0, width, step):
        cols = slice(at, at + step)
        part = jnp.dot(activated, w_down[:, cols], preferred_element_type=jnp.float32) * gate
        core_across_out[:, cols] = part[3 * share :].astype(jnp.bfloat16)
        core_near_out[:, cols] = part[2 * share : 3 * share].astype(jnp.bfloat16)
        across_out[:, cols] = part[share : 2 * share]
        near_out[:, cols] = part[:share]


def expert_half(tail, expert, blocks, w_gate, w_up, w_down):
    share, width = blocks[0].shape[0], w_gate.shape[0]
    wide = jax.ShapeDtypeStruct((share, width), jnp.float32)
    sent = jax.ShapeDtypeStruct((share, width), jnp.bfloat16)
    return pl.pallas_call(
        functools.partial(expert_kernel, tail),
        out_shape=(wide, wide, sent, sent),
        in_specs=[SM] + [VM] * 7,
        out_specs=(VM,) * 4,
        compiler_params=pltpu.CompilerParams(vmem_limit_bytes=40 * MIB),
        name="expert_half",
    )(expert, *blocks, w_gate, w_up, w_down)


def all_tokens(tail, residual, payload, position, w_gate, w_up, w_down):
    seqs = payload.shape[0]
    devices = lax.axis_size("expert")
    far = range(4, devices, 4)
    near = jnp.concatenate([payload] + [swap(payload, "expert", f) for f in far], 0)
    across = swap(near, "expert", 2)
    core_near = swap(near, "expert", 1)
    core_across = swap(across, "expert", 1)
    expert = position // 2
    near_sum, across_sum, core_near_part, core_across_part = expert_half(
        tail, expert, (near, across, core_near, core_across), w_gate, w_up, w_down
    )
    across_sum = across_sum + swap(core_across_part, "expert", 1).astype(jnp.float32)
    near_sum = near_sum + swap(core_near_part, "expert", 1).astype(jnp.float32)
    near_sum = near_sum + swap(across_sum.astype(jnp.bfloat16), "expert", 2).astype(jnp.float32)
    total = residual.astype(jnp.float32) + near_sum[:seqs]
    for at, f in enumerate(far):
        piece = near_sum[(at + 1) * seqs : (at + 2) * seqs].astype(jnp.bfloat16)
        total = total + swap(piece, "expert", f).astype(jnp.float32)
    return total.astype(jnp.bfloat16)


def local(
    hidden_in,
    queries,
    decode_key_value,
    local_kv,
    page_table,
    seq_blocks,
    prompt_kv,
    prompt_owner,
    prompt_pages,
    norm_gain,
    router,
    w_gate,
    w_up,
    w_down,
    route_ids,
):
    devices = lax.axis_size("expert")
    position = lax.axis_index("expert")
    experts = devices // 2
    seq_dev = hidden_in.shape[0]
    key_value_width = KEY_VALUE_HEADS * HEAD_SIZE
    capacity = min(seq_dev, max(2, 2 * ((3 * seq_dev * TOPK + 2 * devices - 1) // (2 * devices))))
    half_cap = capacity // 2
    even_core = position % 2 == 0
    dense = capacity >= seq_dev and devices >= 4 and devices & (devices - 1) == 0
    tail = 2 * (-(-experts // 64) * 64) if dense else 0
    here = position.astype(jnp.int32).reshape(1)
    outgoing = pack(prompt_owner, prompt_kv[0], devices)
    arrived = lax.all_to_all(
        outgoing.reshape(devices, MAXP, 2, PAGE_TOKENS, key_value_width),
        "expert",
        split_axis=0,
        concat_axis=0,
        tiled=True,
    )
    old = local_attention(seq_blocks, queries, decode_key_value, local_kv, page_table)
    residual, normed, spread = finish_heads(
        tail,
        here,
        prompt_owner,
        prompt_pages,
        queries,
        decode_key_value,
        arrived,
        old,
        hidden_in,
        norm_gain.reshape(1, D),
        router,
        route_ids,
    )
    if dense:
        return all_tokens(tail, residual, normed, here, w_gate[0], w_up[0], w_down[0])
    resid_wide = residual.astype(jnp.float32)
    expert_onehot = route_ids[:, :, None] == jnp.arange(experts, dtype=jnp.int32)[None, None, :]
    gate_weights = jnp.sum(jnp.where(expert_onehot, spread[:, None, :], 0.0), -1)
    assigned = seq_dev * TOPK
    expert_ids = route_ids.reshape(assigned)
    chosen = (expert_ids[:, None] == jnp.arange(experts, dtype=jnp.int32)[None, :]).astype(
        jnp.int32
    )
    before = jnp.cumsum(chosen, 0) - chosen
    slot_rank = jnp.sum(before * chosen, 1)
    slot_index = expert_ids * capacity + slot_rank
    placing = slot_index[None, :] == jnp.arange(experts * capacity, dtype=jnp.int32)[:, None]
    selector = jnp.any(placing.reshape(experts * capacity, seq_dev, TOPK), -1).astype(jnp.bfloat16)
    gathered_rows = jnp.dot(selector, normed, preferred_element_type=jnp.float32).astype(
        jnp.bfloat16
    )
    outgoing_half = gathered_rows.reshape(devices, half_cap, D)
    own_half = lax.all_to_all(outgoing_half, "expert", split_axis=0, concat_axis=0, tiled=True)
    partner_half = partner(own_half, "expert", 0)
    received = jnp.where(
        even_core,
        jnp.concatenate([own_half, partner_half], 1),
        jnp.concatenate([partner_half, own_half], 1),
    )
    flattened = received.reshape(devices * capacity, D)
    gate_proj = jnp.dot(flattened, w_gate[0], preferred_element_type=jnp.float32)
    up_proj = jnp.dot(flattened, w_up[0], preferred_element_type=jnp.float32)
    activated = (jax.nn.silu(gate_proj) * up_proj).astype(jnp.bfloat16)
    partial_value = jnp.dot(activated, w_down[0], preferred_element_type=jnp.float32).reshape(
        devices, capacity, D
    )
    kept = jnp.where(even_core, partial_value[:, :half_cap], partial_value[:, half_cap:])
    handed = jnp.where(even_core, partial_value[:, half_cap:], partial_value[:, :half_cap])
    partner_part = partner(handed, "expert", 0)
    finished = (kept + partner_part).astype(jnp.bfloat16)
    returned = lax.all_to_all(finished, "expert", split_axis=0, concat_axis=0, tiled=True)
    expert_sum = returned.reshape(experts * capacity, D)
    picked = jnp.take(expert_sum, slot_index, axis=0).astype(jnp.float32).reshape(seq_dev, TOPK, D)
    expert_mix = jnp.sum(picked * gate_weights[:, :, None], 1)
    return (resid_wide + expert_mix).astype(jnp.bfloat16)


def solution(mesh):
    return jax.shard_map(
        local,
        mesh=mesh,
        in_specs=(
            P(("groups", "expert"), None),
            P(("groups", "expert"), None),
            P(("groups", "expert"), None, None),
            P(("groups", "expert"), None, None, None),
            P(("groups", "expert"), None),
            P(("groups", "expert")),
            P(("groups", "expert"), None, None, None, None),
            P("groups"),
            P("groups"),
            P(),
            P(),
            P("expert", None, None),
            P("expert", None, None),
            P("expert", None, None),
            P(("groups", "expert"), None),
        ),
        out_specs=P(("groups", "expert"), None),
        check_vma=False,
    )
```

time: 111 us -> 74.9 us (0.67)
  blocking collectives: 20.3 us -> 0 us
  waiting for transfers between devices: 18.4 us -> 36.6 us
  other arithmetic: 16.7 us -> 0.83 us
  matrix products: 15.7 us -> 0 us
  local copies, waits for them, and re-layouts: 26.4 us -> 11.6 us
  Pallas kernels: 0 us -> 7.46 us
  starting transfers between devices: 12 us -> 17.7 us
    ppermute x2 -> x12, waiting for transfers between devices: 4.88 us -> 28 us  [swap(): lax.ppermute(x, axis, [(i, i ^ offset) for i in range(lax.axis_size(axis))])]
    all_to_all x1 -> x0, blocking collectives: 20.3 us -> none  [local(): lax.all_to_all(outgoing_half, 'expert', split_axis=0, concat_axis=0, tile...]
    dot_general x10 -> x0, matrix products: 15.7 us -> none  [the longest x1 5.82 us: local(): jnp.dot(activated, w_down[0], preferred_element_type=jnp.float32)]
    ppermute x2 -> x12, starting transfers between devices: 0.29 us -> 10.3 us  [swap(): lax.ppermute(x, axis, [(i, i ^ offset) for i in range(lax.axis_size(axis))])]
    gather x4 -> x0, local copies, waits for them, and re-layouts: 9.3 us -> none  [the longest x1 3.27 us: local(): jnp.take(expert_sum, slot_index, axis=0).astype(jnp.float32)]
    unnamed x25 -> x38, local copies, waits for them, and re-layouts: 3.14 us -> 11.6 us
    pallas_call x0 -> x4, Pallas kernels: none -> 7.46 us  [the longest x1 2.59 us: finish_heads(): pl.pallas_call(functools.partial(head_kernel, tail), out_shape=(jax.Shape...]
    another operation x4 -> x0, local copies, waits for them, and re-layouts: 5.91 us -> none  [the longest x2 2.97 us: attend(): rows_of_keys.reshape(decode_tokens, -1, KEY_VALUE_HEADS, HEAD_SIZE)]
  transfers between devices with their start and end apart: 4 -> 13, of which waited for: 3 -> 10; matrix products, arithmetic and copies ran while one was open for 15% -> 2% of each run, Pallas kernels for 0% -> 2%
where the time goes in v2:
time: 74.9 us; the launch traced here: 74.4 us
  waiting for transfers between devices  36.6 us (49%)
  starting transfers between devices  17.7 us (24%)
  local copies, waits for them, and re-layouts  11.6 us (15%)
  Pallas kernels  7.46 us (10%)
  other arithmetic  0.83 us (1%)
    ppermute x12, waiting for transfers between devices, swap(): lax.ppermute(x, axis, [(i, i ^ offset) for i in range(lax.axis_size(axis))])  28 us
    unnamed x38, local copies, waits for them, and re-layouts  11.6 us
    ppermute x12, starting transfers between devices, swap(): lax.ppermute(x, axis, [(i, i ^ offset) for i in range(lax.axis_size(axis))])  10.3 us
    all_to_all x1, waiting for transfers between devices, local(): lax.all_to_all(outgoing.reshape(devices, MAXP, 2, PAGE_TOKENS, key_value_...  8.63 us
    all_to_all x1, starting transfers between devices, local(): lax.all_to_all(outgoing.reshape(devices, MAXP, 2, PAGE_TOKENS, key_value_...  7.41 us
    pallas_call x1, Pallas kernels, finish_heads(): pl.pallas_call(functools.partial(head_kernel, tail), out_shape=(jax.Shape...  2.59 us
    pallas_call x1, Pallas kernels, expert_half(): pl.pallas_call(functools.partial(expert_kernel, tail), out_shape=(wide, w...  1.92 us
    pallas_call x1, Pallas kernels, pack(): pl.pallas_call(pack_kernel, out_shape=jax.ShapeDtypeStruct((devices * MAX...  1.53 us
  transfers between devices with their start and end apart: 13, of which 10 were waited for; matrix products, arithmetic and copies ran while one was open for 2% of the time, Pallas kernels for 2%

profile of v2, /device:TPU:0, one launch (start us, length us, event | category | flops | bytes accessed | tf_op | source)
XLA Modules:
  0.0 74.4 jit_solution(11175741532304115865)
XLA Ops:
  1.7 1.5 %pack_pages.1 = bf16[32,2,16,256]{3,2,1,0:T(8,128)(2,1)} custom-call(s32[16]{0:T(128)S(1)} %copy-done.13, bf16[16,2,16,256]{3,2,1,0:T(8,128)(2,1)S(1)} %bitcast.10), custom_call_target="tpu_custom_call" | custom-call | tf_op jit(solution)/shard_map/pack_pages/pallas_call | solution.py:68
  3.2 7.4 %all-to-all-start = ((bf16[16,2,2,16,256]{4,3,2,1,0:T(8,128)(2,1)}), bf16[16,2,2,16,256]{4,3,2,1,0:T(8,128)(2,1)S(1)}, u32[]{:S(2)}, u32[]{:S(2)}) async-start(bf16[16,2,2,16,256]{4,3,2,1,0:T(8,128)(2,1)} %bitcast.2), calls=%async_computation | async-start | bytes 1048576 | tf_op jit(solution)/shard_map/all_to_all | solution.py:340
  10.7 1.3 %copy.16.router = bf16[4096,8]{1,0:T(8,128)(2,1)S(1)} copy(bf16[4096,8]{0,1:T(8,128)(2,1)} %param.25) | data formatting | bytes 131072 | tf_op args[10]
  14.9 1.4 %local_attention.1.old = bf16[8,4096]{1,0:T(8,128)(2,1)S(1)} custom-call(s32[8]{0:T(128)S(1)} %copy-done.15, bf16[8,4096]{1,0:T(8,128)(2,1)S(1)} %copy-done.5, bf16[8,2,256]{2,1,0:T(2,128)(2,1)S(1)} %copy-done.8, bf16[32,2,16,256]{3,2,1,0:T(8,128)(2,1)S(1)} %copy-done.3, s32[8,16]{1,0:T(8,128)S(1)} %copy-done.11), custom_call_target="tpu_custom_call" | custom-call | tf_op jit(solution)/shard_map/local_attention/pallas_call | solution.py:142
  16.3 8.6 %all-to-all-done.arrived = bf16[16,2,2,16,256]{4,3,2,1,0:T(8,128)(2,1)S(1)} async-done(((bf16[16,2,2,16,256]{4,3,2,1,0:T(8,128)(2,1)}), bf16[16,2,2,16,256]{4,3,2,1,0:T(8,128)(2,1)S(1)}, u32[]{:S(2)}, u32[]{:S(2)}) %all-to-all-start) | async-done | bytes 524320 | tf_op jit(solution)/shard_map/all_to_all | solution.py:340
  25.0 2.6 %finish_heads.1 = (bf16[8,4096]{1,0:T(8,128)(2,1)S(1)}, bf16[8,4224]{1,0:T(8,128)(2,1)S(1)}, f32[8,8]{1,0:T(8,128)}) custom-call(s32[1]{0:T(128)} %bitcast.position, s32[16]{0:T(128)S(1)} %copy-done.14, s32[16]{0:T(128)S(1)} %copy-done.16, bf16[8,4096]{1,0:T(8,128)(2,1)S(1)} %copy-done.6, bf16[8,2,256]{2,1,0:T(2,128)(2,1)S(1)} %copy-done.9, ...), custom_call_target="tpu_custom_call" | custom-call | tf_op jit(solution)/shard_map/finish_heads/pallas_call | solution.py:233
  27.6 1.5 %collective-permute-start.2 = (bf16[8,4224]{1,0:T(8,128)(2,1)S(1)}, bf16[8,4224]{1,0:T(8,128)(2,1)S(1)}, u32[]{:S(2)}, u32[]{:S(2)}) collective-permute-start(bf16[8,4224]{1,0:T(8,128)(2,1)S(1)} %get-tuple-element.12), channel_id=1, source_target_pairs={{0,12},{1,13},{2,14},{3,15},{4,8},{5,9},{6,10},{7,11},{8,4},{9,5},... | collective-permute-start | bytes 202760 | tf_op jit(solution)/shard_map/ppermute | solution.py:30
  29.0 1.1 %collective-permute-start.1 = (bf16[8,4224]{1,0:T(8,128)(2,1)S(1)}, bf16[8,4224]{1,0:T(8,128)(2,1)S(1)}, u32[]{:S(2)}, u32[]{:S(2)}) collective-permute-start(bf16[8,4224]{1,0:T(8,128)(2,1)S(1)} %get-tuple-element.12), channel_id=1, source_target_pairs={{0,8},{1,9},{2,10},{3,11},{4,12},{5,13},{6,14},{7,15},{8,0},{9,1},... | collective-permute-start | bytes 202760 | tf_op jit(solution)/shard_map/ppermute | solution.py:30
  30.2 1.8 %collective-permute-start = (bf16[8,4224]{1,0:T(8,128)(2,1)S(1)}, bf16[8,4224]{1,0:T(8,128)(2,1)S(1)}, u32[]{:S(2)}, u32[]{:S(2)}) collective-permute-start(bf16[8,4224]{1,0:T(8,128)(2,1)S(1)} %get-tuple-element.12), channel_id=1, source_target_pairs={{0,4},{1,5},{2,6},{3,7},{4,0},{5,1},{6,2},{7,3},{8,12},{9,13},{10,... | collective-permute-start | bytes 202760 | tf_op jit(solution)/shard_map/ppermute | solution.py:30
  32.0 3.2 %collective-permute-done = bf16[8,4224]{1,0:T(8,128)(2,1)S(1)} collective-permute-done((bf16[8,4224]{1,0:T(8,128)(2,1)S(1)}, bf16[8,4224]{1,0:T(8,128)(2,1)S(1)}, u32[]{:S(2)}, u32[]{:S(2)}) %collective-permute-start) | collective-permute-done | bytes 67616 | tf_op jit(solution)/shard_map/ppermute | solution.py:30
  35.1 2.1 %collective-permute-done.1 = bf16[8,4224]{1,0:T(8,128)(2,1)S(1)} collective-permute-done((bf16[8,4224]{1,0:T(8,128)(2,1)S(1)}, bf16[8,4224]{1,0:T(8,128)(2,1)S(1)}, u32[]{:S(2)}, u32[]{:S(2)}) %collective-permute-start.1) | collective-permute-done | bytes 67616 | tf_op jit(solution)/shard_map/ppermute | solution.py:30
  38.3 7.4 %collective-permute-done.3.across = bf16[32,4224]{1,0:T(8,128)(2,1)S(1)} collective-permute-done((bf16[32,4224]{1,0:T(8,128)(2,1)S(1)}, bf16[32,4224]{1,0:T(8,128)(2,1)S(1)}, u32[]{:S(2)}, u32[]{:S(2)}) %collective-permute-start.3) | collective-permute-done | bytes 270368 | tf_op jit(solution)/shard_map/ppermute | solution.py:30
  45.7 1.5 %collective-permute-done.5.core_across = bf16[32,4224]{1,0:T(8,128)(2,1)S(1)} collective-permute-done((bf16[32,4224]{1,0:T(8,128)(2,1)S(1)}, bf16[32,4224]{1,0:T(8,128)(2,1)S(1)}, u32[]{:S(2)}, u32[]{:S(2)}) %collective-permute-start.5) | collective-permute-done | bytes 270368 | tf_op jit(solution)/shard_map/ppermute | solution.py:30
  47.2 1.9 %copy-done = bf16[1,4096,384]{2,1,0:T(8,128)(2,1)S(1)} copy-done((bf16[1,4096,384]{2,1,0:T(8,128)(2,1)S(1)}, bf16[1,4096,384]{2,1,0:T(8,128)(2,1)}, u32[]{:S(2)}) %copy-start) | copy-done | bytes 3145752
  49.1 1.9 %copy-done.1 = bf16[1,4096,384]{2,1,0:T(8,128)(2,1)S(1)} copy-done((bf16[1,4096,384]{2,1,0:T(8,128)(2,1)S(1)}, bf16[1,4096,384]{2,1,0:T(8,128)(2,1)}, u32[]{:S(2)}) %copy-start.1) | copy-done | bytes 3145752
  51.0 1.9 %copy-done.2 = bf16[1,384,4096]{2,1,0:T(8,128)(2,1)S(1)} copy-done((bf16[1,384,4096]{2,1,0:T(8,128)(2,1)S(1)}, bf16[1,384,4096]{2,1,0:T(8,128)(2,1)}, u32[]{:S(2)}) %copy-start.2) | copy-done | bytes 3145752
  52.9 1.9 %expert_half.1 = (f32[32,4096]{1,0:T(8,128)S(1)}, f32[32,4096]{1,0:T(8,128)S(1)}, bf16[32,4096]{1,0:T(8,128)(2,1)S(1)}, bf16[32,4096]{1,0:T(8,128)(2,1)S(1)}) custom-call(s32[1]{0:T(128)S(6)} %select_n.5.expert, bf16[32,4224]{1,0:T(8,128)(2,1)S(1)} %constant_dynamic-update-slice_fusion.near, bf16[32,4224]{1,0:T(8,128)(2,1)S(1)} %collective-permute-done.3.across, ...), custom_call_target="tpu_custom_call" | custom-call | tf_op jit(solution)/shard_map/expert_half/pallas_call | solution.py:279
  55.4 1.0 %collective-permute-done.7 = bf16[32,4096]{1,0:T(8,128)(2,1)S(1)} collective-permute-done((bf16[32,4096]{1,0:T(8,128)(2,1)S(1)}, bf16[32,4096]{1,0:T(8,128)(2,1)S(1)}, u32[]{:S(2)}, u32[]{:S(2)}) %collective-permute-start.7) | collective-permute-done | bytes 262176 | tf_op jit(solution)/shard_map/ppermute | solution.py:30
  57.3 7.6 %collective-permute-done.8 = bf16[32,4096]{1,0:T(8,128)(2,1)S(1)} collective-permute-done((bf16[32,4096]{1,0:T(8,128)(2,1)S(1)}, bf16[32,4096]{1,0:T(8,128)(2,1)S(1)}, u32[]{:S(2)}, u32[]{:S(2)}) %collective-permute-start.8) | collective-permute-done | bytes 262176 | tf_op jit(solution)/shard_map/ppermute | solution.py:30
  65.1 1.5 %collective-permute-start.11 = (bf16[8,4096]{1,0:T(8,128)(2,1)S(1)}, bf16[8,4096]{1,0:T(8,128)(2,1)S(1)}, u32[]{:S(2)}, u32[]{:S(2)}) collective-permute-start(bf16[8,4096]{1,0:T(8,128)(2,1)S(1)} %get-tuple-element.20), channel_id=1, source_target_pairs={{0,12},{1,13},{2,14},{3,15},{4,8},{5,9},{6,10},{7,11},{8,4},{9,5},... | collective-permute-start | bytes 196616 | tf_op jit(solution)/shard_map/ppermute | solution.py:30
  66.6 2.0 %collective-permute-start.10 = (bf16[8,4096]{1,0:T(8,128)(2,1)S(1)}, bf16[8,4096]{1,0:T(8,128)(2,1)S(1)}, u32[]{:S(2)}, u32[]{:S(2)}) collective-permute-start(bf16[8,4096]{1,0:T(8,128)(2,1)S(1)} %get-tuple-element.21), channel_id=1, source_target_pairs={{0,8},{1,9},{2,10},{3,11},{4,12},{5,13},{6,14},{7,15},{8,0},{9,1},... | collective-permute-start | bytes 196616 | tf_op jit(solution)/shard_map/ppermute | solution.py:30
  68.6 1.6 %collective-permute-done.9 = bf16[8,4096]{1,0:T(8,128)(2,1)S(1)} collective-permute-done((bf16[8,4096]{1,0:T(8,128)(2,1)S(1)}, bf16[8,4096]{1,0:T(8,128)(2,1)S(1)}, u32[]{:S(2)}, u32[]{:S(2)}) %collective-permute-start.9) | collective-permute-done | bytes 65568 | tf_op jit(solution)/shard_map/ppermute | solution.py:30
  70.1 1.1 %collective-permute-done.11 = bf16[8,4096]{1,0:T(8,128)(2,1)S(1)} collective-permute-done((bf16[8,4096]{1,0:T(8,128)(2,1)S(1)}, bf16[8,4096]{1,0:T(8,128)(2,1)S(1)}, u32[]{:S(2)}, u32[]{:S(2)}) %collective-permute-start.11) | collective-permute-done | bytes 65568 | tf_op jit(solution)/shard_map/ppermute | solution.py:30
  71.2 2.5 %collective-permute-done.10 = bf16[8,4096]{1,0:T(8,128)(2,1)S(1)} collective-permute-done((bf16[8,4096]{1,0:T(8,128)(2,1)S(1)}, bf16[8,4096]{1,0:T(8,128)(2,1)S(1)}, u32[]{:S(2)}, u32[]{:S(2)}) %collective-permute-start.10) | collective-permute-done | bytes 65568 | tf_op jit(solution)/shard_map/ppermute | solution.py:30
  (49 shorter events, 7.9 us)
Async XLA Ops:
  0.0 12.0 %copy-start.3 = (bf16[32,2,16,256]{3,2,1,0:T(8,128)(2,1)S(1)}, bf16[32,2,16,256]{3,2,1,0:T(8,128)(2,1)}, u32[]{:S(2)}) copy-start(bf16[32,2,16,256]{3,2,1,0:T(8,128)(2,1)} %pool.1) | copy-start | bytes 1572868
  1.7 23.3 %copy-start.6 = (bf16[8,4096]{1,0:T(8,128)(2,1)S(1)}, bf16[8,4096]{1,0:T(8,128)(2,1)}, u32[]{:S(2)}) copy-start(bf16[8,4096]{1,0:T(8,128)(2,1)} %queries.3) | copy-start | bytes 196612
  1.7 23.3 %copy-start.7 = (bf16[8,4096]{1,0:T(8,128)(2,1)S(1)}, bf16[8,4096]{1,0:T(8,128)(2,1)}, u32[]{:S(2)}) copy-start(bf16[8,4096]{1,0:T(8,128)(2,1)} %hidden.1) | copy-start | bytes 196612
  1.7 23.3 %copy-start.9 = (bf16[8,2,256]{2,1,0:T(2,128)(2,1)S(1)}, bf16[8,2,256]{2,1,0:T(2,128)(2,1)}, u32[]{:S(2)}) copy-start(bf16[8,2,256]{2,1,0:T(2,128)(2,1)} %own_kv.3) | copy-start | bytes 24580
  1.7 23.3 %copy-start.10 = (f32[4096]{0:T(1024)S(1)}, f32[4096]{0:T(1024)}, u32[]{:S(2)}) copy-start(f32[4096]{0:T(1024)} %param.24) | copy-start | bytes 49156
  1.7 23.3 %copy-start.12 = (s32[8,8]{1,0:T(8,128)S(1)}, s32[8,8]{1,0:T(8,128)}, u32[]{:S(2)}) copy-start(s32[8,8]{1,0:T(8,128)} %routes.1) | copy-start | bytes 772
  1.7 23.3 %copy-start.14 = (s32[16]{0:T(128)S(1)}, s32[16]{0:T(128)}, u32[]{:S(2)}) copy-start(s32[16]{0:T(128)} %owner.3) | copy-start | bytes 196
  1.7 23.3 %copy-start.16 = (s32[16]{0:T(128)S(1)}, s32[16]{0:T(128)}, u32[]{:S(2)}) copy-start(s32[16]{0:T(128)} %lengths.1) | copy-start | bytes 196
  3.2 21.7 %all-to-all-start = ((bf16[16,2,2,16,256]{4,3,2,1,0:T(8,128)(2,1)}), bf16[16,2,2,16,256]{4,3,2,1,0:T(8,128)(2,1)S(1)}, u32[]{:S(2)}, u32[]{:S(2)}) async-start(bf16[16,2,2,16,256]{4,3,2,1,0:T(8,128)(2,1)} %bitcast.2), calls=%async_computation | async-start | bytes 1048576 | tf_op jit(solution)/shard_map/all_to_all | solution.py:340
  27.6 9.7 %collective-permute-start.2 = (bf16[8,4224]{1,0:T(8,128)(2,1)S(1)}, bf16[8,4224]{1,0:T(8,128)(2,1)S(1)}, u32[]{:S(2)}, u32[]{:S(2)}) collective-permute-start(bf16[8,4224]{1,0:T(8,128)(2,1)S(1)} %get-tuple-element.12), channel_id=1, source_target_pairs={{0,12},{1,13},{2,14},{3,15},{4,8},{5,9},{6,10},{7,11},{8,4},{9,5},... | collective-permute-start | bytes 202760 | tf_op jit(solution)/shard_map/ppermute | solution.py:30
  29.0 8.3 %collective-permute-start.1 = (bf16[8,4224]{1,0:T(8,128)(2,1)S(1)}, bf16[8,4224]{1,0:T(8,128)(2,1)S(1)}, u32[]{:S(2)}, u32[]{:S(2)}) collective-permute-start(bf16[8,4224]{1,0:T(8,128)(2,1)S(1)} %get-tuple-element.12), channel_id=1, source_target_pairs={{0,8},{1,9},{2,10},{3,11},{4,12},{5,13},{6,14},{7,15},{8,0},{9,1},... | collective-permute-start | bytes 202760 | tf_op jit(solution)/shard_map/ppermute | solution.py:30
  30.2 5.0 %collective-permute-start = (bf16[8,4224]{1,0:T(8,128)(2,1)S(1)}, bf16[8,4224]{1,0:T(8,128)(2,1)S(1)}, u32[]{:S(2)}, u32[]{:S(2)}) collective-permute-start(bf16[8,4224]{1,0:T(8,128)(2,1)S(1)} %get-tuple-element.12), channel_id=1, source_target_pairs={{0,4},{1,5},{2,6},{3,7},{4,0},{5,1},{6,2},{7,3},{8,12},{9,13},{10,... | collective-permute-start | bytes 202760 | tf_op jit(solution)/shard_map/ppermute | solution.py:30
  37.3 8.3 %collective-permute-start.3 = (bf16[32,4224]{1,0:T(8,128)(2,1)S(1)}, bf16[32,4224]{1,0:T(8,128)(2,1)S(1)}, u32[]{:S(2)}, u32[]{:S(2)}) collective-permute-start(bf16[32,4224]{1,0:T(8,128)(2,1)S(1)} %constant_dynamic-update-slice_fusion.near), channel_id=1, source_target_pairs={{0,2},{1,3},{2,0},{3,1},{4,6},{5,7},{6,4},{7,5},{8,10},{9,11},{10,... | collective-permute-start | bytes 811016 | tf_op jit(solution)/shard_map/ppermute | solution.py:30
  38.3 7.4 %collective-permute-start.4 = (bf16[32,4224]{1,0:T(8,128)(2,1)S(1)}, bf16[32,4224]{1,0:T(8,128)(2,1)S(1)}, u32[]{:S(2)}, u32[]{:S(2)}) collective-permute-start(bf16[32,4224]{1,0:T(8,128)(2,1)S(1)} %constant_dynamic-update-slice_fusion.near), channel_id=1, source_target_pairs={{0,1},{1,0},{2,3},{3,2},{4,5},{5,4},{6,7},{7,6},{8,9},{9,8},{10,11... | collective-permute-start | bytes 811016 | tf_op jit(solution)/shard_map/ppermute | solution.py:30
  45.7 1.5 %collective-permute-start.5 = (bf16[32,4224]{1,0:T(8,128)(2,1)S(1)}, bf16[32,4224]{1,0:T(8,128)(2,1)S(1)}, u32[]{:S(2)}, u32[]{:S(2)}) collective-permute-start(bf16[32,4224]{1,0:T(8,128)(2,1)S(1)} %collective-permute-done.3.across), channel_id=1, source_target_pairs={{0,1},{1,0},{2,3},{3,2},{4,5},{5,4},{6,7},{7,6},{8,9},{9,8},{10,11... | collective-permute-start | bytes 811016 | tf_op jit(solution)/shard_map/ppermute | solution.py:30
  47.2 1.9 %copy-start = (bf16[1,4096,384]{2,1,0:T(8,128)(2,1)S(1)}, bf16[1,4096,384]{2,1,0:T(8,128)(2,1)}, u32[]{:S(2)}) copy-start(bf16[1,4096,384]{2,1,0:T(8,128)(2,1)} %param.26) | copy-start | bytes 9437188
  49.1 1.9 %copy-start.1 = (bf16[1,4096,384]{2,1,0:T(8,128)(2,1)S(1)}, bf16[1,4096,384]{2,1,0:T(8,128)(2,1)}, u32[]{:S(2)}) copy-start(bf16[1,4096,384]{2,1,0:T(8,128)(2,1)} %param.27) | copy-start | bytes 9437188
  51.0 1.9 %copy-start.2 = (bf16[1,384,4096]{2,1,0:T(8,128)(2,1)S(1)}, bf16[1,384,4096]{2,1,0:T(8,128)(2,1)}, u32[]{:S(2)}) copy-start(bf16[1,384,4096]{2,1,0:T(8,128)(2,1)} %param.28) | copy-start | bytes 9437188
  54.8 1.6 %collective-permute-start.7 = (bf16[32,4096]{1,0:T(8,128)(2,1)S(1)}, bf16[32,4096]{1,0:T(8,128)(2,1)S(1)}, u32[]{:S(2)}, u32[]{:S(2)}) collective-permute-start(bf16[32,4096]{1,0:T(8,128)(2,1)S(1)} %get-tuple-element.16), channel_id=1, source_target_pairs={{0,1},{1,0},{2,3},{3,2},{4,5},{5,4},{6,7},{7,6},{8,9},{9,8},{10,11... | collective-permute-start | bytes 786440 | tf_op jit(solution)/shard_map/ppermute | solution.py:30
  55.0 2.3 %collective-permute-start.6 = (bf16[32,4096]{1,0:T(8,128)(2,1)S(1)}, bf16[32,4096]{1,0:T(8,128)(2,1)S(1)}, u32[]{:S(2)}, u32[]{:S(2)}) collective-permute-start(bf16[32,4096]{1,0:T(8,128)(2,1)S(1)} %get-tuple-element.14), channel_id=1, source_target_pairs={{0,1},{1,0},{2,3},{3,2},{4,5},{5,4},{6,7},{7,6},{8,9},{9,8},{10,11... | collective-permute-start | bytes 786440 | tf_op jit(solution)/shard_map/ppermute | solution.py:30
  56.5 8.4 %collective-permute-start.8 = (bf16[32,4096]{1,0:T(8,128)(2,1)S(1)}, bf16[32,4096]{1,0:T(8,128)(2,1)S(1)}, u32[]{:S(2)}, u32[]{:S(2)}) collective-permute-start(bf16[32,4096]{1,0:T(8,128)(2,1)S(1)} %add_convert_fusion), channel_id=1, source_target_pairs={{0,2},{1,3},{2,0},{3,1},{4,6},{5,7},{6,4},{7,5},{8,10},{9,11},{10,... | collective-permute-start | bytes 786440 | tf_op jit(solution)/shard_map/ppermute | solution.py:30
  65.0 5.1 %collective-permute-start.9 = (bf16[8,4096]{1,0:T(8,128)(2,1)S(1)}, bf16[8,4096]{1,0:T(8,128)(2,1)S(1)}, u32[]{:S(2)}, u32[]{:S(2)}) collective-permute-start(bf16[8,4096]{1,0:T(8,128)(2,1)S(1)} %get-tuple-element.19), channel_id=1, source_target_pairs={{0,4},{1,5},{2,6},{3,7},{4,0},{5,1},{6,2},{7,3},{8,12},{9,13},{10,... | collective-permute-start | bytes 196616 | tf_op jit(solution)/shard_map/ppermute | solution.py:30
  65.1 6.1 %collective-permute-start.11 = (bf16[8,4096]{1,0:T(8,128)(2,1)S(1)}, bf16[8,4096]{1,0:T(8,128)(2,1)S(1)}, u32[]{:S(2)}, u32[]{:S(2)}) collective-permute-start(bf16[8,4096]{1,0:T(8,128)(2,1)S(1)} %get-tuple-element.20), channel_id=1, source_target_pairs={{0,12},{1,13},{2,14},{3,15},{4,8},{5,9},{6,10},{7,11},{8,4},{9,5},... | collective-permute-start | bytes 196616 | tf_op jit(solution)/shard_map/ppermute | solution.py:30
  66.6 7.1 %collective-permute-start.10 = (bf16[8,4096]{1,0:T(8,128)(2,1)S(1)}, bf16[8,4096]{1,0:T(8,128)(2,1)S(1)}, u32[]{:S(2)}, u32[]{:S(2)}) collective-permute-start(bf16[8,4096]{1,0:T(8,128)(2,1)S(1)} %get-tuple-element.21), channel_id=1, source_target_pairs={{0,8},{1,9},{2,10},{3,11},{4,12},{5,13},{6,14},{7,15},{8,0},{9,1},... | collective-permute-start | bytes 196616 | tf_op jit(solution)/shard_map/ppermute | solution.py:30
  (6 other events, 4.5 us)

commit v3 on v2

--- a/solution.py
+++ b/solution.py
@@ -34,11 +34,16 @@
     return pl.BlockSpec(memory_space=space)
 
 
-VM, SM = whole(pltpu.VMEM), whole(pltpu.SMEM)
+VM, SM, ANY = whole(pltpu.VMEM), whole(pltpu.SMEM), whole(pl.ANY)
 MIB = 1 << 20
 
 
-def pack_kernel(owner, pages, out, source, count):
+def pack_kernel(owner_in, pages_in, out, owner, pages, source, count, sems):
+    fetch_owner = pltpu.make_async_copy(owner_in, owner, sems.at[0])
+    fetch_pages = pltpu.make_async_copy(pages_in, pages, sems.at[1])
+    fetch_owner.start()
+    fetch_pages.start()
+
     def clear(i, _):
         source[i] = 0
         return 0
@@ -60,7 +65,9 @@
 
     lax.fori_loop(0, source.shape[0], clear, 0, unroll=8)
     lax.fori_loop(0, count.shape[0], clear_count, 0, unroll=8)
+    fetch_owner.wait()
     lax.fori_loop(0, owner.shape[0], place, 0, unroll=8)
+    fetch_pages.wait()
     lax.fori_loop(0, out.shape[0], move, 0, unroll=8)
 
 
@@ -68,9 +75,15 @@
     return pl.pallas_call(
         pack_kernel,
         out_shape=jax.ShapeDtypeStruct((devices * MAXP,) + pages.shape[1:], pages.dtype),
-        in_specs=[SM, VM],
+        in_specs=[ANY, ANY],
         out_specs=VM,
-        scratch_shapes=[pltpu.SMEM((devices * MAXP,), jnp.int32), pltpu.SMEM((devices,), jnp.int32)],
+        scratch_shapes=[
+            pltpu.SMEM(prompt_owner.shape, jnp.int32),
+            pltpu.VMEM(pages.shape, pages.dtype),
+            pltpu.SMEM((devices * MAXP,), jnp.int32),
+            pltpu.SMEM((devices,), jnp.int32),
+            pltpu.SemaphoreType.DMA((2,)),
+        ],
         compiler_params=pltpu.CompilerParams(vmem_limit_bytes=16 * MIB),
         name="pack_pages",
     )(prompt_owner, pages)
@@ -110,9 +123,53 @@
     )
 
 
-def local_kernel(blocks, queries, own_kv, pool, table, out):
+def own_prompts(position, owner, lengths):
+    here = position[0]
+
+    def find(p, carry):
+        found = carry[0]
+        mine = owner[p] == here
+        picked = [jnp.where(mine & (found == r), lengths[p], carry[1 + r]) for r in range(MAXP)]
+        return (jnp.where(mine, found + 1, found), *picked)
+
+    state = lax.fori_loop(0, owner.shape[0], find, (jnp.int32(0),) * (1 + MAXP), unroll=8)
+    return state[0], state[1:]
+
+
+def normalize(tail, mixed, keep, gain, router, routes, residual, payload, spread):
+    seqs, width = mixed.shape
+    rows = residual.shape[0]
+    experts = router.shape[1]
+    summed = mixed[...].astype(jnp.bfloat16)
+    wide = summed.astype(jnp.float32)
+    residual[...] = jnp.where(keep, wide, 0.0).astype(jnp.bfloat16)[:rows]
+    level = lax.rsqrt(jnp.mean(wide * wide, -1, keepdims=True) + norm_eps)
+    normed = (wide * level * gain[...]).astype(jnp.bfloat16)
+    payload[:, :width] = normed[:rows]
+    logits = jnp.dot(normed, router[...], preferred_element_type=jnp.float32)
+    lane = lax.broadcasted_iota(jnp.int32, (seqs, experts), 1)
+    chosen = jnp.zeros((seqs, experts), jnp.float32)
+    for k in range(routes.shape[1]):
+        chosen = chosen + jnp.where(routes[:, k : k + 1] == lane, 1.0, 0.0)
+    top = jnp.max(jnp.where(chosen > 0.0, logits, masked_score), -1, keepdims=True)
+    powers = jnp.where(chosen > 0.0, jnp.exp(logits - top), 0.0) * chosen
+    gates = jnp.where(keep, powers / jnp.sum(powers, -1, keepdims=True), 0.0)
+    spread[...] = gates[:rows]
+    if tail:
+        payload[:, width:] = jnp.zeros((rows, tail), jnp.bfloat16)
+        coarse = gates.astype(jnp.bfloat16)
+        fine = (gates - coarse.astype(jnp.float32)).astype(jnp.bfloat16)
+        payload[:, width : width + experts] = coarse[:rows]
+        payload[:, width + tail // 2 : width + tail // 2 + experts] = fine[:rows]
+
+
+def old_kernel(
+    tail, position, owner, lengths, blocks, queries, own_kv, pool, table, hidden, gain, router, routes,
+    residual, payload, spread, mixed,
+):
     seqs = queries.shape[0]
     tokens = pool.shape[0] * PAGE_TOKENS
+    new_count, _ = own_prompts(position, owner, lengths)
     page = lax.broadcasted_iota(jnp.int32, (seqs, tokens), 1) // PAGE_TOKENS
     row = lax.broadcasted_iota(jnp.int32, (seqs, 1), 0)
     limit = jnp.zeros((seqs, 1), jnp.int32)
@@ -134,53 +191,24 @@
             own_kv[:, 1, cols].astype(jnp.float32),
         )
         for j in range(group):
-            at = (g * group + j) * HEAD_SIZE
-            out[:, at : at + HEAD_SIZE] = result[j].astype(jnp.bfloat16)
-
-
-def local_attention(seq_blocks, queries, own_kv, pool, page_table):
-    return pl.pallas_call(
-        local_kernel,
-        out_shape=jax.ShapeDtypeStruct(queries.shape, jnp.bfloat16),
-        in_specs=[SM, VM, VM, VM, VM],
-        out_specs=VM,
-        compiler_params=pltpu.CompilerParams(vmem_limit_bytes=16 * MIB),
-        name="local_attention",
-    )(seq_blocks, queries, own_kv, pool, page_table)
-
-
-def head_kernel(
-    tail, position, owner, lengths, queries, own_kv, arrived, old, hidden, gain, router, routes,
+            at = slice((g * group + j) * HEAD_SIZE, (g * group + j + 1) * HEAD_SIZE)
+            rounded = result[j].astype(jnp.bfloat16).astype(jnp.float32)
+            mixed[:, at] = hidden[:, at].astype(jnp.float32) + rounded
+    normalize(tail, mixed, row >= new_count, gain, router, routes, residual, payload, spread)
+
+
+def fresh_kernel(
+    tail, position, owner, lengths, queries, own_kv, arrived, hidden, gain, router, routes,
     residual, payload, spread, mixed,
 ):
     seqs = queries.shape[0]
-    width = queries.shape[1]
-    experts = router.shape[1]
     tokens = arrived.shape[0] * PAGE_TOKENS
-    here = position[0]
-
-    def find(p, carry):
-        found = carry[0]
-        mine = owner[p] == here
-        picked = [
-            jnp.where(mine & (found == r), lengths[p], carry[1 + r]) for r in range(MAXP)
-        ]
-        return (jnp.where(mine, found + 1, found), *picked)
-
-    state = lax.fori_loop(
-        0, owner.shape[0], find, (jnp.int32(0),) * (1 + MAXP), unroll=8
-    )
-    new_count = state[0]
+    new_count, pages = own_prompts(position, owner, lengths)
     row = lax.broadcasted_iota(jnp.int32, (seqs, 1), 0)
     page = lax.broadcasted_iota(jnp.int32, (seqs, tokens), 1) // PAGE_TOKENS
     counts = jnp.concatenate(
-        [
-            jnp.where((page < state[1 + r]) & (row == r), 1.0, 0.0)
-            for r in range(MAXP)
-        ],
-        1,
-    )
-    is_new = row < new_count
+        [jnp.where((page < pages[r]) & (row == r), 1.0, 0.0) for r in range(MAXP)], 1
+    )
     group = QUERY_HEADS // KEY_VALUE_HEADS
     for g in range(KEY_VALUE_HEADS):
         cols = slice(g * HEAD_SIZE, (g + 1) * HEAD_SIZE)
@@ -200,112 +228,145 @@
         )
         for j in range(group):
             at = slice((g * group + j) * HEAD_SIZE, (g * group + j + 1) * HEAD_SIZE)
-            fresh = result[j].astype(jnp.bfloat16).astype(jnp.float32)
-            chosen = jnp.where(is_new, fresh, old[:, at].astype(jnp.float32))
-            mixed[:, at] = hidden[:, at].astype(jnp.float32) + chosen
-    summed = mixed[...].astype(jnp.bfloat16)
-    residual[...] = summed
-    wide = summed.astype(jnp.float32)
-    level = lax.rsqrt(jnp.mean(wide * wide, -1, keepdims=True) + norm_eps)
-    normed = (wide * level * gain[...]).astype(jnp.bfloat16)
-    payload[:, :width] = normed
-    logits = jnp.dot(normed, router[...], preferred_element_type=jnp.float32)
-    lane = lax.broadcasted_iota(jnp.int32, (seqs, experts), 1)
-    chosen = jnp.zeros((seqs, experts), jnp.float32)
-    for k in range(routes.shape[1]):
-        chosen = chosen + jnp.where(routes[:, k : k + 1] == lane, 1.0, 0.0)
-    top = jnp.max(jnp.where(chosen > 0.0, logits, masked_score), -1, keepdims=True)
-    powers = jnp.where(chosen > 0.0, jnp.exp(logits - top), 0.0) * chosen
-    gates = powers / jnp.sum(powers, -1, keepdims=True)
-    spread[...] = gates
-    if tail:
-        payload[:, width:] = jnp.zeros((seqs, tail), jnp.bfloat16)
-        coarse = gates.astype(jnp.bfloat16)
-        payload[:, width : width + experts] = coarse
-        fine = (gates - coarse.astype(jnp.float32)).astype(jnp.bfloat16)
-        payload[:, width + tail // 2 : width + tail // 2 + experts] = fine
-
-
-def finish_heads(
-    tail, position, prompt_owner, prompt_pages, queries, own_kv, arrived, old, hidden, gain, router, routes
-):
-    seqs, width = queries.shape
+            rounded = result[j].astype(jnp.bfloat16).astype(jnp.float32)
+            mixed[:, at] = hidden[:, at].astype(jnp.float32) + rounded
+    normalize(tail, mixed, row < new_count, gain, router, routes, residual, payload, spread)
+
+
+def heads(kernel, name, tail, rows, experts, scalars, arrays):
+    seqs, width = arrays[0].shape
     return pl.pallas_call(
-        functools.partial(head_kernel, tail),
+        functools.partial(kernel, tail),
         out_shape=(
-            jax.ShapeDtypeStruct((seqs, width), jnp.bfloat16),
-            jax.ShapeDtypeStruct((seqs, width + tail), jnp.bfloat16),
-            jax.ShapeDtypeStruct((seqs, router.shape[1]), jnp.float32),
+            jax.ShapeDtypeStruct((rows, width), jnp.bfloat16),
+            jax.ShapeDtypeStruct((rows, width + tail), jnp.bfloat16),
+            jax.ShapeDtypeStruct((rows, experts), jnp.float32),
         ),
-        in_specs=[SM, SM, SM] + [VM] * 8,
+        in_specs=[SM] * len(scalars) + [VM] * len(arrays),
         out_specs=(VM, VM, VM),
         scratch_shapes=[pltpu.VMEM((seqs, width), jnp.float32)],
         compiler_params=pltpu.CompilerParams(vmem_limit_bytes=32 * MIB),
-        name="finish_heads",
-    )(
-        position, prompt_owner, prompt_pages, queries, own_kv, arrived, old, hidden, gain, router, routes
-    )
-
-
-def expert_kernel(
-    tail, expert, near, across, core_near, core_across, w_gate, w_up, w_down,
-    near_out, across_out, core_near_out, core_across_out,
-):
-    width = w_gate.shape[0]
-    share = near.shape[0]
-    blocks = (near, across, core_near, core_across)
-    tokens = jnp.concatenate([block[:, :width] for block in blocks], 0)
+        name=name,
+    )(*scalars, *arrays)
+
+
+def expert_rows(tail, expert, blocks, gate_up, down, outs):
+    near_out, across_out, core_near_out, core_across_out = outs
+    share, width = near_out.shape
     ends = jnp.concatenate([block[:, width:].astype(jnp.float32) for block in blocks], 0)
     lane = lax.broadcasted_iota(jnp.int32, ends.shape, 1)
     wanted = (lane == expert[0]) | (lane == expert[0] + tail // 2)
     gate = jnp.sum(jnp.where(wanted, ends, 0.0), -1, keepdims=True)
-    gate_proj = jnp.dot(tokens, w_gate[...], preferred_element_type=jnp.float32)
-    up_proj = jnp.dot(tokens, w_up[...], preferred_element_type=jnp.float32)
+    gate_proj, up_proj = gate_up(
+        lambda cols: jnp.concatenate([block[:, cols] for block in blocks], 0)
+    )
     activated = (gate_proj / (1.0 + jnp.exp(-gate_proj)) * up_proj).astype(jnp.bfloat16)
     step = min(width, 1024)
     for at in range(0, width, step):
         cols = slice(at, at + step)
-        part = jnp.dot(activated, w_down[:, cols], preferred_element_type=jnp.float32) * gate
+        part = jnp.dot(activated, down(cols), preferred_element_type=jnp.float32) * gate
         core_across_out[:, cols] = part[3 * share :].astype(jnp.bfloat16)
         core_near_out[:, cols] = part[2 * share : 3 * share].astype(jnp.bfloat16)
         across_out[:, cols] = part[share : 2 * share]
         near_out[:, cols] = part[:share]
 
 
-def expert_half(tail, expert, blocks, w_gate, w_up, w_down):
-    share, width = blocks[0].shape[0], w_gate.shape[0]
+PIECES = 4
+
+
+def first_expert_kernel(
+    tail, expert, near, across, core_near, core_across, gate_in, up_in, down_in,
+    near_out, across_out, core_near_out, core_across_out, w_gate, w_up, w_down, sems,
+):
+    width, hidden = w_gate.shape
+    part = width // PIECES
+    copies = {}
+    for at in range(PIECES):
+        rows = pl.ds(at * part, part)
+        for i, (src, dst) in enumerate(((gate_in, w_gate), (up_in, w_up))):
+            copies[i, at] = pltpu.make_async_copy(src.at[rows], dst.at[rows], sems.at[i, at])
+    for at in range(PIECES):
+        rows = pl.ds(at * (hidden // PIECES), hidden // PIECES)
+        copies[2, at] = pltpu.make_async_copy(down_in.at[rows], w_down.at[rows], sems.at[2, at])
+    for copy in copies.values():
+        copy.start()
+
+    def gate_up(tokens):
+        gate_proj = up_proj = 0.0
+        for at in range(PIECES):
+            cols = slice(at * part, (at + 1) * part)
+            x = tokens(cols)
+            copies[0, at].wait()
+            gate_proj = gate_proj + jnp.dot(x, w_gate[cols], preferred_element_type=jnp.float32)
+            copies[1, at].wait()
+            up_proj = up_proj + jnp.dot(x, w_up[cols], preferred_element_type=jnp.float32)
+        for at in range(PIECES):
+            copies[2, at].wait()
+        return gate_proj, up_proj
+
+    expert_rows(
+        tail, expert, (near, across, core_near, core_across), gate_up,
+        lambda cols: w_down[:, cols],
+        (near_out, across_out, core_near_out, core_across_out),
+    )
+
+
+def later_expert_kernel(
+    tail, expert, near, across, core_near, core_across, w_gate, w_up, w_down,
+    near_out, across_out, core_near_out, core_across_out,
+):
+    def gate_up(tokens):
+        x = tokens(slice(0, w_gate.shape[0]))
+        return (
+            jnp.dot(x, w_gate[...], preferred_element_type=jnp.float32),
+            jnp.dot(x, w_up[...], preferred_element_type=jnp.float32),
+        )
+
+    expert_rows(
+        tail, expert, (near, across, core_near, core_across), gate_up,
+        lambda cols: w_down[:, cols],
+        (near_out, across_out, core_near_out, core_across_out),
+    )
+
+
+def expert_half(first, tail, expert, blocks, weights):
+    share, width = blocks[0].shape[0], weights[0].shape[0]
     wide = jax.ShapeDtypeStruct((share, width), jnp.float32)
     sent = jax.ShapeDtypeStruct((share, width), jnp.bfloat16)
+    kept = tuple(jax.ShapeDtypeStruct(w.shape, w.dtype) for w in weights) if first else ()
     return pl.pallas_call(
-        functools.partial(expert_kernel, tail),
-        out_shape=(wide, wide, sent, sent),
-        in_specs=[SM] + [VM] * 7,
-        out_specs=(VM,) * 4,
-        compiler_params=pltpu.CompilerParams(vmem_limit_bytes=40 * MIB),
-        name="expert_half",
-    )(expert, *blocks, w_gate, w_up, w_down)
-
-
-def all_tokens(tail, residual, payload, position, w_gate, w_up, w_down):
-    seqs = payload.shape[0]
-    devices = lax.axis_size("expert")
-    far = range(4, devices, 4)
-    near = jnp.concatenate([payload] + [swap(payload, "expert", f) for f in far], 0)
+        functools.partial(first_expert_kernel if first else later_expert_kernel, tail),
+        out_shape=(wide, wide, sent, sent) + kept,
+        in_specs=[SM] + [VM] * 4 + [ANY if first else VM] * 3,
+        out_specs=(VM,) * (4 + len(kept)),
+        scratch_shapes=[pltpu.SemaphoreType.DMA((3, PIECES))] if first else [],
+        compiler_params=pltpu.CompilerParams(vmem_limit_bytes=32 * MIB),
+        name="first_expert" if first else "later_expert",
+    )(expert, *blocks, *weights)
+
+
+def far_peers():
+    return range(4, lax.axis_size("expert"), 4)
+
+
+def gather_tokens(payload):
+    near = jnp.concatenate([payload] + [swap(payload, "expert", f) for f in far_peers()], 0)
     across = swap(near, "expert", 2)
     core_near = swap(near, "expert", 1)
     core_across = swap(across, "expert", 1)
-    expert = position // 2
-    near_sum, across_sum, core_near_part, core_across_part = expert_half(
-        tail, expert, (near, across, core_near, core_across), w_gate, w_up, w_down
-    )
+    return near, across, core_near, core_across
+
+
+def scatter_sums(residual, near_sum, across_sum, core_near_part, core_across_part):
+    seqs = residual.shape[0]
     across_sum = across_sum + swap(core_across_part, "expert", 1).astype(jnp.float32)
     near_sum = near_sum + swap(core_near_part, "expert", 1).astype(jnp.float32)
     near_sum = near_sum + swap(across_sum.astype(jnp.bfloat16), "expert", 2).astype(jnp.float32)
     total = residual.astype(jnp.float32) + near_sum[:seqs]
-    for at, f in enumerate(far):
+    for at, f in enumerate(far_peers()):
         piece = near_sum[(at + 1) * seqs : (at + 2) * seqs].astype(jnp.bfloat16)
         total = total + swap(piece, "expert", f).astype(jnp.float32)
-    return total.astype(jnp.bfloat16)
+    return total
 
 
 def local(
@@ -344,23 +405,41 @@
         concat_axis=0,
         tiled=True,
     )
-    old = local_attention(seq_blocks, queries, decode_key_value, local_kv, page_table)
-    residual, normed, spread = finish_heads(
+    scalars = (here, prompt_owner, prompt_pages)
+    gain = norm_gain.reshape(1, D)
+    old_residual, old_rows, old_spread = heads(
+        old_kernel,
+        "old_heads",
         tail,
-        here,
-        prompt_owner,
-        prompt_pages,
-        queries,
-        decode_key_value,
-        arrived,
-        old,
-        hidden_in,
-        norm_gain.reshape(1, D),
-        router,
-        route_ids,
+        seq_dev,
+        experts,
+        scalars + (seq_blocks,),
+        (queries, decode_key_value, local_kv, page_table, hidden_in, gain, router, route_ids),
+    )
+    new_residual, new_rows, new_spread = heads(
+        fresh_kernel,
+        "new_heads",
+        tail,
+        MAXP,
+        experts,
+        scalars,
+        (queries, decode_key_value, arrived, hidden_in, gain, router, route_ids),
     )
     if dense:
-        return all_tokens(tail, residual, normed, here, w_gate[0], w_up[0], w_down[0])
+        expert = here // 2
+        old_parts = expert_half(
+            True, tail, expert, gather_tokens(old_rows), (w_gate[0], w_up[0], w_down[0])
+        )
+        new_parts = expert_half(False, tail, expert, gather_tokens(new_rows), old_parts[4:])
+        old_total = scatter_sums(old_residual, *old_parts[:4])
+        new_total = scatter_sums(new_residual, *new_parts)
+        return (old_total + jnp.pad(new_total, ((0, seq_dev - MAXP), (0, 0)))).astype(jnp.bfloat16)
+    rest = ((0, seq_dev - MAXP), (0, 0))
+    new_count = jnp.sum((prompt_owner == position).astype(jnp.int32))
+    is_new = jnp.arange(seq_dev, dtype=jnp.int32)[:, None] < new_count
+    residual = old_residual + jnp.pad(new_residual, rest)
+    normed = jnp.where(is_new, jnp.pad(new_rows, rest), old_rows)
+    spread = old_spread + jnp.pad(new_spread, rest)
     resid_wide = residual.astype(jnp.float32)
     expert_onehot = route_ids[:, :, None] == jnp.arange(experts, dtype=jnp.int32)[None, None, :]
     gate_weights = jnp.sum(jnp.where(expert_onehot, spread[:, None, :], 0.0), -1)

time: 74.9 us -> 89.6 us (1.20)
  starting transfers between devices: 17.7 us -> 29.3 us
  waiting for transfers between devices: 36.6 us -> 30.7 us
  Pallas kernels: 7.46 us -> 12 us
  local copies, waits for them, and re-layouts: 11.6 us -> 15.6 us
    ppermute x12 -> x24, starting transfers between devices: 10.3 us -> 23.1 us  [swap(): lax.ppermute(x, axis, [(i, i ^ offset) for i in range(lax.axis_size(axis))])]
    all_to_all x1, waiting for transfers between devices: 8.63 us -> 0.01 us  [local(): lax.all_to_all(outgoing.reshape(devices, MAXP, 2, PAGE_TOKENS, key_value_...]
    pallas_call x3 -> x4, Pallas kernels: 5.93 us -> 10.5 us  [the longest x2 5.42 us: expert_half(): pl.pallas_call(functools.partial(first_expert_kernel if first else later_...]
    unnamed x38 -> x46, local copies, waits for them, and re-layouts: 11.6 us -> 15.6 us
    ppermute x12 -> x24, waiting for transfers between devices: 28 us -> 30.7 us  [swap(): lax.ppermute(x, axis, [(i, i ^ offset) for i in range(lax.axis_size(axis))])]
    all_to_all x1, starting transfers between devices: 7.41 us -> 6.16 us  [local(): lax.all_to_all(outgoing.reshape(devices, MAXP, 2, PAGE_TOKENS, key_value_...]
  transfers between devices with their start and end apart: 13 -> 25, of which waited for: 10 -> 10; matrix products, arithmetic and copies ran while one was open for 2% -> 0% of each run, Pallas kernels for 2% -> 11%
where the time goes in v3:
time: 89.6 us; the launch traced here: 88.9 us
  waiting for transfers between devices  30.7 us (34%)
  starting transfers between devices  29.3 us (33%)
  local copies, waits for them, and re-layouts  15.6 us (17%)
  Pallas kernels  12 us (13%)
  other arithmetic  1 us (1%)
    ppermute x24, waiting for transfers between devices, swap(): lax.ppermute(x, axis, [(i, i ^ offset) for i in range(lax.axis_size(axis))])  30.7 us
    ppermute x24, starting transfers between devices, swap(): lax.ppermute(x, axis, [(i, i ^ offset) for i in range(lax.axis_size(axis))])  23.1 us
    unnamed x46, local copies, waits for them, and re-layouts  15.6 us
    all_to_all x1, starting transfers between devices, local(): lax.all_to_all(outgoing.reshape(devices, MAXP, 2, PAGE_TOKENS, key_value_...  6.16 us
    pallas_call x2, Pallas kernels, expert_half(): pl.pallas_call(functools.partial(first_expert_kernel if first else later_...  5.42 us
    pallas_call x2, Pallas kernels, heads(): pl.pallas_call(functools.partial(kernel, tail), out_shape=(jax.ShapeDtype...  5.11 us
  transfers between devices with their start and end apart: 25, of which 10 were waited for; matrix products, arithmetic and copies ran while one was open for 0% of the time, Pallas kernels for 11%

profile of v3, /device:TPU:0, one launch (start us, length us, event | category | flops | bytes accessed | tf_op | source)
XLA Modules:
  0.0 88.9 jit_solution(14843150772088931429)
XLA Ops:
  0.0 1.4 %copy.16.router = bf16[4096,8]{1,0:T(8,128)(2,1)S(1)} copy(bf16[4096,8]{0,1:T(8,128)(2,1)} %param.25) | data formatting | bytes 131072 | tf_op args[10]
  1.5 1.0 %copy-done.3 = bf16[32,2,16,256]{3,2,1,0:T(8,128)(2,1)S(1)} copy-done((bf16[32,2,16,256]{3,2,1,0:T(8,128)(2,1)S(1)}, bf16[32,2,16,256]{3,2,1,0:T(8,128)(2,1)}, u32[]{:S(2)}) %copy-start.3) | copy-done | bytes 524312
  8.9 2.5 %old_heads.1 = (bf16[8,4096]{1,0:T(8,128)(2,1)S(1)}, bf16[8,4224]{1,0:T(8,128)(2,1)S(1)}, f32[8,8]{1,0:T(8,128)}) custom-call(s32[1]{0:T(128)} %bitcast.position, s32[16]{0:T(128)S(1)} %copy-done.15, s32[16]{0:T(128)S(1)} %copy-done.18, s32[8]{0:T(128)S(1)} %copy-done.20, bf16[8,4096]{1,0:T(8,128)(2,1)S(1)} %copy-done.5, bf16[8,2,256]{2,1,0:T(2,128)(2,1)S(1)} %copy-done.11, ...), custom_call_target="tpu_custom_call" | custom-call | tf_op jit(solution)/shard_map/old_heads/pallas_call | solution.py:238
  11.5 5.1 %collective-permute-start.2 = (bf16[8,4224]{1,0:T(8,128)(2,1)S(1)}, bf16[8,4224]{1,0:T(8,128)(2,1)S(1)}, u32[]{:S(2)}, u32[]{:S(2)}) collective-permute-start(bf16[8,4224]{1,0:T(8,128)(2,1)S(1)} %get-tuple-element.21), channel_id=1, source_target_pairs={{0,12},{1,13},{2,14},{3,15},{4,8},{5,9},{6,10},{7,11},{8,4},{9,5},... | collective-permute-start | bytes 202760 | tf_op jit(solution)/shard_map/ppermute | solution.py:30
  18.1 1.5 %pack_pages.1 = bf16[32,2,16,256]{3,2,1,0:T(8,128)(2,1)} custom-call(s32[16]{0:T(128)S(1)} %copy-done.15, bf16[16,2,16,256]{3,2,1,0:T(8,128)(2,1)S(1)} %bitcast.10), custom_call_target="tpu_custom_call" | custom-call | tf_op jit(solution)/shard_map/pack_pages/pallas_call | solution.py:75
  19.6 6.2 %all-to-all-start = ((bf16[16,2,2,16,256]{4,3,2,1,0:T(8,128)(2,1)}), bf16[16,2,2,16,256]{4,3,2,1,0:T(8,128)(2,1)S(1)}, u32[]{:S(2)}, u32[]{:S(2)}) async-start(bf16[16,2,2,16,256]{4,3,2,1,0:T(8,128)(2,1)} %bitcast.6), calls=%async_computation | async-start | bytes 1048576 | tf_op jit(solution)/shard_map/all_to_all | solution.py:401
  25.9 2.0 %collective-permute-start.3 = (bf16[32,4224]{1,0:T(8,128)(2,1)S(1)}, bf16[32,4224]{1,0:T(8,128)(2,1)S(1)}, u32[]{:S(2)}, u32[]{:S(2)}) collective-permute-start(bf16[32,4224]{1,0:T(8,128)(2,1)S(1)} %constant_dynamic-update-slice_fusion.near), channel_id=1, source_target_pairs={{0,2},{1,3},{2,0},{3,1},{4,6},{5,7},{6,4},{7,5},{8,10},{9,11},{10,... | collective-permute-start | bytes 811016 | tf_op jit(solution)/shard_map/ppermute | solution.py:30
  27.9 12.3 %collective-permute-done.3.across = bf16[32,4224]{1,0:T(8,128)(2,1)S(1)} collective-permute-done((bf16[32,4224]{1,0:T(8,128)(2,1)S(1)}, bf16[32,4224]{1,0:T(8,128)(2,1)S(1)}, u32[]{:S(2)}, u32[]{:S(2)}) %collective-permute-start.3) | collective-permute-done | bytes 270368 | tf_op jit(solution)/shard_map/ppermute | solution.py:30
  40.2 2.6 %new_heads.1 = (bf16[2,4096]{1,0:T(2,128)(2,1)S(1)}, bf16[2,4224]{1,0:T(2,128)(2,1)S(1)}, f32[2,8]{1,0:T(2,128)}) custom-call(s32[1]{0:T(128)} %bitcast.position, s32[16]{0:T(128)S(1)} %copy-done.16, s32[16]{0:T(128)S(1)} %copy-done.19, bf16[8,4096]{1,0:T(8,128)(2,1)S(1)} %copy-done.6, bf16[8,2,256]{2,1,0:T(2,128)(2,1)S(1)} %copy-done.12, ...), custom_call_target="tpu_custom_call" | custom-call | tf_op jit(solution)/shard_map/new_heads/pallas_call | solution.py:238
  42.8 3.4 %collective-permute-start.14 = (bf16[2,4224]{1,0:T(2,128)(2,1)S(1)}, bf16[2,4224]{1,0:T(2,128)(2,1)S(1)}, u32[]{:S(2)}, u32[]{:S(2)}) collective-permute-start(bf16[2,4224]{1,0:T(2,128)(2,1)S(1)} %get-tuple-element.27), channel_id=1, source_target_pairs={{0,12},{1,13},{2,14},{3,15},{4,8},{5,9},{6,10},{7,11},{8,4},{9,5},... | collective-permute-start | bytes 50696 | tf_op jit(solution)/shard_map/ppermute | solution.py:30
  47.2 1.9 %copy-done = bf16[1,4096,384]{2,1,0:T(8,128)(2,1)S(1)} copy-done((bf16[1,4096,384]{2,1,0:T(8,128)(2,1)S(1)}, bf16[1,4096,384]{2,1,0:T(8,128)(2,1)}, u32[]{:S(2)}) %copy-start) | copy-done | bytes 3145752
  49.1 1.9 %copy-done.1 = bf16[1,4096,384]{2,1,0:T(8,128)(2,1)S(1)} copy-done((bf16[1,4096,384]{2,1,0:T(8,128)(2,1)S(1)}, bf16[1,4096,384]{2,1,0:T(8,128)(2,1)}, u32[]{:S(2)}) %copy-start.1) | copy-done | bytes 3145752
  51.0 1.9 %copy-done.2 = bf16[1,384,4096]{2,1,0:T(8,128)(2,1)S(1)} copy-done((bf16[1,384,4096]{2,1,0:T(8,128)(2,1)S(1)}, bf16[1,384,4096]{2,1,0:T(8,128)(2,1)}, u32[]{:S(2)}) %copy-start.2) | copy-done | bytes 3145752
  52.9 3.8 %first_expert.1 = (f32[32,4096]{1,0:T(8,128)S(1)}, f32[32,4096]{1,0:T(8,128)S(1)}, bf16[32,4096]{1,0:T(8,128)(2,1)S(1)}, bf16[32,4096]{1,0:T(8,128)(2,1)S(1)}, b...) custom-call(s32[1]{0:T(128)S(6)} %select_n.5.expert, ...), custom_call_target="tpu_custom_call" | custom-call | tf_op jit(solution)/shard_map/first_expert/pallas_call | solution.py:337
  57.5 4.0 %collective-permute-done.15.across = bf16[8,4224]{1,0:T(8,128)(2,1)S(1)} collective-permute-done((bf16[8,4224]{1,0:T(8,128)(2,1)S(1)}, bf16[8,4224]{1,0:T(8,128)(2,1)S(1)}, u32[]{:S(2)}, u32[]{:S(2)}) %collective-permute-start.15) | collective-permute-done | bytes 67616 | tf_op jit(solution)/shard_map/ppermute | solution.py:30
  62.7 1.7 %later_expert.1 = (f32[8,4096]{1,0:T(8,128)S(1)}, f32[8,4096]{1,0:T(8,128)S(1)}, bf16[8,4096]{1,0:T(8,128)(2,1)S(1)}, bf16[8,4096]{1,0:T(8,128)(2,1)S(1)}) custom-call(s32[1]{0:T(128)S(6)} %select_n.5.expert, bf16[8,4224]{1,0:T(8,128)(2,1)S(1)} %pad_maximum_fusion.near, bf16[8,4224]{1,0:T(8,128)(2,1)S(1)} %collective-permute-done.15.across, ...), custom_call_target="tpu_custom_call" | custom-call | tf_op jit(solution)/shard_map/later_expert/pallas_call | solution.py:337
  65.7 1.2 %collective-permute-start.20 = (bf16[8,4096]{1,0:T(8,128)(2,1)S(1)}, bf16[8,4096]{1,0:T(8,128)(2,1)S(1)}, u32[]{:S(2)}, u32[]{:S(2)}) collective-permute-start(bf16[8,4096]{1,0:T(8,128)(2,1)S(1)} %add_convert_fusion.1), channel_id=1, source_target_pairs={{0,2},{1,3},{2,0},{3,1},{4,6},{5,7},{6,4},{7,5},{8,10},{9,11},{10,... | collective-permute-start | bytes 196616 | tf_op jit(solution)/shard_map/ppermute | solution.py:30
  66.9 7.0 %collective-permute-done.8 = bf16[32,4096]{1,0:T(8,128)(2,1)S(1)} collective-permute-done((bf16[32,4096]{1,0:T(8,128)(2,1)S(1)}, bf16[32,4096]{1,0:T(8,128)(2,1)S(1)}, u32[]{:S(2)}, u32[]{:S(2)}) %collective-permute-start.8) | collective-permute-done | bytes 262176 | tf_op jit(solution)/shard_map/ppermute | solution.py:30
  74.8 1.1 %collective-permute-start.21 = (bf16[2,4096]{1,0:T(2,128)(2,1)S(1)}, bf16[2,4096]{1,0:T(2,128)(2,1)S(1)}, u32[]{:S(2)}, u32[]{:S(2)}) collective-permute-start(bf16[2,4096]{1,0:T(2,128)(2,1)S(1)} %get-tuple-element.42), channel_id=1, source_target_pairs={{0,4},{1,5},{2,6},{3,7},{4,0},{5,1},{6,2},{7,3},{8,12},{9,13},{10,... | collective-permute-start | bytes 49160 | tf_op jit(solution)/shard_map/ppermute | solution.py:30
  75.8 2.4 %collective-permute-start.23 = (bf16[2,4096]{1,0:T(2,128)(2,1)S(1)}, bf16[2,4096]{1,0:T(2,128)(2,1)S(1)}, u32[]{:S(2)}, u32[]{:S(2)}) collective-permute-start(bf16[2,4096]{1,0:T(2,128)(2,1)S(1)} %get-tuple-element.43), channel_id=1, source_target_pairs={{0,12},{1,13},{2,14},{3,15},{4,8},{5,9},{6,10},{7,11},{8,4},{9,5},... | collective-permute-start | bytes 49160 | tf_op jit(solution)/shard_map/ppermute | solution.py:30
  78.8 1.5 %collective-permute-start.9 = (bf16[8,4096]{1,0:T(8,128)(2,1)S(1)}, bf16[8,4096]{1,0:T(8,128)(2,1)S(1)}, u32[]{:S(2)}, u32[]{:S(2)}) collective-permute-start(bf16[8,4096]{1,0:T(8,128)(2,1)S(1)} %get-tuple-element.39), channel_id=1, source_target_pairs={{0,4},{1,5},{2,6},{3,7},{4,0},{5,1},{6,2},{7,3},{8,12},{9,13},{10,... | collective-permute-start | bytes 196616 | tf_op jit(solution)/shard_map/ppermute | solution.py:30
  80.3 2.4 %collective-permute-start.11 = (bf16[8,4096]{1,0:T(8,128)(2,1)S(1)}, bf16[8,4096]{1,0:T(8,128)(2,1)S(1)}, u32[]{:S(2)}, u32[]{:S(2)}) collective-permute-start(bf16[8,4096]{1,0:T(8,128)(2,1)S(1)} %get-tuple-element.40), channel_id=1, source_target_pairs={{0,12},{1,13},{2,14},{3,15},{4,8},{5,9},{6,10},{7,11},{8,4},{9,5},... | collective-permute-start | bytes 196616 | tf_op jit(solution)/shard_map/ppermute | solution.py:30
  84.0 2.5 %collective-permute-done.11 = bf16[8,4096]{1,0:T(8,128)(2,1)S(1)} collective-permute-done((bf16[8,4096]{1,0:T(8,128)(2,1)S(1)}, bf16[8,4096]{1,0:T(8,128)(2,1)S(1)}, u32[]{:S(2)}, u32[]{:S(2)}) %collective-permute-start.11) | collective-permute-done | bytes 65568 | tf_op jit(solution)/shard_map/ppermute | solution.py:30
  86.5 1.7 %collective-permute-done.10 = bf16[8,4096]{1,0:T(8,128)(2,1)S(1)} collective-permute-done((bf16[8,4096]{1,0:T(8,128)(2,1)S(1)}, bf16[8,4096]{1,0:T(8,128)(2,1)S(1)}, u32[]{:S(2)}, u32[]{:S(2)}) %collective-permute-start.10) | collective-permute-done | bytes 65568 | tf_op jit(solution)/shard_map/ppermute | solution.py:30
  (87 shorter events, 15.7 us)
Async XLA Ops:
  11.5 14.3 %collective-permute-start.2 = (bf16[8,4224]{1,0:T(8,128)(2,1)S(1)}, bf16[8,4224]{1,0:T(8,128)(2,1)S(1)}, u32[]{:S(2)}, u32[]{:S(2)}) collective-permute-start(bf16[8,4224]{1,0:T(8,128)(2,1)S(1)} %get-tuple-element.21), channel_id=1, source_target_pairs={{0,12},{1,13},{2,14},{3,15},{4,8},{5,9},{6,10},{7,11},{8,4},{9,5},... | collective-permute-start | bytes 202760 | tf_op jit(solution)/shard_map/ppermute | solution.py:30
  16.6 9.2 %collective-permute-start.1 = (bf16[8,4224]{1,0:T(8,128)(2,1)S(1)}, bf16[8,4224]{1,0:T(8,128)(2,1)S(1)}, u32[]{:S(2)}, u32[]{:S(2)}) collective-permute-start(bf16[8,4224]{1,0:T(8,128)(2,1)S(1)} %get-tuple-element.21), channel_id=1, source_target_pairs={{0,8},{1,9},{2,10},{3,11},{4,12},{5,13},{6,14},{7,15},{8,0},{9,1},... | collective-permute-start | bytes 202760 | tf_op jit(solution)/shard_map/ppermute | solution.py:30
  16.6 9.2 %collective-permute-start = (bf16[8,4224]{1,0:T(8,128)(2,1)S(1)}, bf16[8,4224]{1,0:T(8,128)(2,1)S(1)}, u32[]{:S(2)}, u32[]{:S(2)}) collective-permute-start(bf16[8,4224]{1,0:T(8,128)(2,1)S(1)} %get-tuple-element.21), channel_id=1, source_target_pairs={{0,4},{1,5},{2,6},{3,7},{4,0},{5,1},{6,2},{7,3},{8,12},{9,13},{10,... | collective-permute-start | bytes 202760 | tf_op jit(solution)/shard_map/ppermute | solution.py:30
  19.6 20.6 %all-to-all-start = ((bf16[16,2,2,16,256]{4,3,2,1,0:T(8,128)(2,1)}), bf16[16,2,2,16,256]{4,3,2,1,0:T(8,128)(2,1)S(1)}, u32[]{:S(2)}, u32[]{:S(2)}) async-start(bf16[16,2,2,16,256]{4,3,2,1,0:T(8,128)(2,1)} %bitcast.6), calls=%async_computation | async-start | bytes 1048576 | tf_op jit(solution)/shard_map/all_to_all | solution.py:401
  25.9 14.3 %collective-permute-start.3 = (bf16[32,4224]{1,0:T(8,128)(2,1)S(1)}, bf16[32,4224]{1,0:T(8,128)(2,1)S(1)}, u32[]{:S(2)}, u32[]{:S(2)}) collective-permute-start(bf16[32,4224]{1,0:T(8,128)(2,1)S(1)} %constant_dynamic-update-slice_fusion.near), channel_id=1, source_target_pairs={{0,2},{1,3},{2,0},{3,1},{4,6},{5,7},{6,4},{7,5},{8,10},{9,11},{10,... | collective-permute-start | bytes 811016 | tf_op jit(solution)/shard_map/ppermute | solution.py:30
  27.8 19.3 %collective-permute-start.4 = (bf16[32,4224]{1,0:T(8,128)(2,1)S(1)}, bf16[32,4224]{1,0:T(8,128)(2,1)S(1)}, u32[]{:S(2)}, u32[]{:S(2)}) collective-permute-start(bf16[32,4224]{1,0:T(8,128)(2,1)S(1)} %constant_dynamic-update-slice_fusion.near), channel_id=1, source_target_pairs={{0,1},{1,0},{2,3},{3,2},{4,5},{5,4},{6,7},{7,6},{8,9},{9,8},{10,11... | collective-permute-start | bytes 811016 | tf_op jit(solution)/shard_map/ppermute | solution.py:30
  40.2 7.0 %collective-permute-start.5 = (bf16[32,4224]{1,0:T(8,128)(2,1)S(1)}, bf16[32,4224]{1,0:T(8,128)(2,1)S(1)}, u32[]{:S(2)}, u32[]{:S(2)}) collective-permute-start(bf16[32,4224]{1,0:T(8,128)(2,1)S(1)} %collective-permute-done.3.across), channel_id=1, source_target_pairs={{0,1},{1,0},{2,3},{3,2},{4,5},{5,4},{6,7},{7,6},{8,9},{9,8},{10,11... | collective-permute-start | bytes 811016 | tf_op jit(solution)/shard_map/ppermute | solution.py:30
  42.8 13.9 %collective-permute-start.14 = (bf16[2,4224]{1,0:T(2,128)(2,1)S(1)}, bf16[2,4224]{1,0:T(2,128)(2,1)S(1)}, u32[]{:S(2)}, u32[]{:S(2)}) collective-permute-start(bf16[2,4224]{1,0:T(2,128)(2,1)S(1)} %get-tuple-element.27), channel_id=1, source_target_pairs={{0,12},{1,13},{2,14},{3,15},{4,8},{5,9},{6,10},{7,11},{8,4},{9,5},... | collective-permute-start | bytes 50696 | tf_op jit(solution)/shard_map/ppermute | solution.py:30
  46.2 10.6 %collective-permute-start.13 = (bf16[2,4224]{1,0:T(2,128)(2,1)S(1)}, bf16[2,4224]{1,0:T(2,128)(2,1)S(1)}, u32[]{:S(2)}, u32[]{:S(2)}) collective-permute-start(bf16[2,4224]{1,0:T(2,128)(2,1)S(1)} %get-tuple-element.27), channel_id=1, source_target_pairs={{0,8},{1,9},{2,10},{3,11},{4,12},{5,13},{6,14},{7,15},{8,0},{9,1},... | collective-permute-start | bytes 50696 | tf_op jit(solution)/shard_map/ppermute | solution.py:30
  46.2 10.6 %collective-permute-start.12 = (bf16[2,4224]{1,0:T(2,128)(2,1)S(1)}, bf16[2,4224]{1,0:T(2,128)(2,1)S(1)}, u32[]{:S(2)}, u32[]{:S(2)}) collective-permute-start(bf16[2,4224]{1,0:T(2,128)(2,1)S(1)} %get-tuple-element.27), channel_id=1, source_target_pairs={{0,4},{1,5},{2,6},{3,7},{4,0},{5,1},{6,2},{7,3},{8,12},{9,13},{10,... | collective-permute-start | bytes 50696 | tf_op jit(solution)/shard_map/ppermute | solution.py:30
  56.6 7.9 %collective-permute-start.7 = (bf16[32,4096]{1,0:T(8,128)(2,1)S(1)}, bf16[32,4096]{1,0:T(8,128)(2,1)S(1)}, u32[]{:S(2)}, u32[]{:S(2)}) collective-permute-start(bf16[32,4096]{1,0:T(8,128)(2,1)S(1)} %get-tuple-element.25), channel_id=1, source_target_pairs={{0,1},{1,0},{2,3},{3,2},{4,5},{5,4},{6,7},{7,6},{8,9},{9,8},{10,11... | collective-permute-start | bytes 786440 | tf_op jit(solution)/shard_map/ppermute | solution.py:30
  56.8 4.6 %collective-permute-start.15 = (bf16[8,4224]{1,0:T(8,128)(2,1)S(1)}, bf16[8,4224]{1,0:T(8,128)(2,1)S(1)}, u32[]{:S(2)}, u32[]{:S(2)}) collective-permute-start(bf16[8,4224]{1,0:T(8,128)(2,1)S(1)} %pad_maximum_fusion.near), channel_id=1, source_target_pairs={{0,2},{1,3},{2,0},{3,1},{4,6},{5,7},{6,4},{7,5},{8,10},{9,11},{10,... | collective-permute-start | bytes 202760 | tf_op jit(solution)/shard_map/ppermute | solution.py:30
  57.3 4.7 %collective-permute-start.16 = (bf16[8,4224]{1,0:T(8,128)(2,1)S(1)}, bf16[8,4224]{1,0:T(8,128)(2,1)S(1)}, u32[]{:S(2)}, u32[]{:S(2)}) collective-permute-start(bf16[8,4224]{1,0:T(8,128)(2,1)S(1)} %pad_maximum_fusion.near), channel_id=1, source_target_pairs={{0,1},{1,0},{2,3},{3,2},{4,5},{5,4},{6,7},{7,6},{8,9},{9,8},{10,11... | collective-permute-start | bytes 202760 | tf_op jit(solution)/shard_map/ppermute | solution.py:30
  61.4 5.5 %collective-permute-start.6 = (bf16[32,4096]{1,0:T(8,128)(2,1)S(1)}, bf16[32,4096]{1,0:T(8,128)(2,1)S(1)}, u32[]{:S(2)}, u32[]{:S(2)}) collective-permute-start(bf16[32,4096]{1,0:T(8,128)(2,1)S(1)} %get-tuple-element.23), channel_id=1, source_target_pairs={{0,1},{1,0},{2,3},{3,2},{4,5},{5,4},{6,7},{7,6},{8,9},{9,8},{10,11... | collective-permute-start | bytes 786440 | tf_op jit(solution)/shard_map/ppermute | solution.py:30
  64.3 1.3 %collective-permute-start.19 = (bf16[8,4096]{1,0:T(8,128)(2,1)S(1)}, bf16[8,4096]{1,0:T(8,128)(2,1)S(1)}, u32[]{:S(2)}, u32[]{:S(2)}) collective-permute-start(bf16[8,4096]{1,0:T(8,128)(2,1)S(1)} %get-tuple-element.34), channel_id=1, source_target_pairs={{0,1},{1,0},{2,3},{3,2},{4,5},{5,4},{6,7},{7,6},{8,9},{9,8},{10,11... | collective-permute-start | bytes 196616 | tf_op jit(solution)/shard_map/ppermute | solution.py:30
  64.6 9.2 %collective-permute-start.8 = (bf16[32,4096]{1,0:T(8,128)(2,1)S(1)}, bf16[32,4096]{1,0:T(8,128)(2,1)S(1)}, u32[]{:S(2)}, u32[]{:S(2)}) collective-permute-start(bf16[32,4096]{1,0:T(8,128)(2,1)S(1)} %add_convert_fusion), channel_id=1, source_target_pairs={{0,2},{1,3},{2,0},{3,1},{4,6},{5,7},{6,4},{7,5},{8,10},{9,11},{10,... | collective-permute-start | bytes 786440 | tf_op jit(solution)/shard_map/ppermute | solution.py:30
  65.0 9.0 %collective-permute-start.18 = (bf16[8,4096]{1,0:T(8,128)(2,1)S(1)}, bf16[8,4096]{1,0:T(8,128)(2,1)S(1)}, u32[]{:S(2)}, u32[]{:S(2)}) collective-permute-start(bf16[8,4096]{1,0:T(8,128)(2,1)S(1)} %get-tuple-element.32), channel_id=1, source_target_pairs={{0,1},{1,0},{2,3},{3,2},{4,5},{5,4},{6,7},{7,6},{8,9},{9,8},{10,11... | collective-permute-start | bytes 196616 | tf_op jit(solution)/shard_map/ppermute | solution.py:30
  65.7 9.0 %collective-permute-start.20 = (bf16[8,4096]{1,0:T(8,128)(2,1)S(1)}, bf16[8,4096]{1,0:T(8,128)(2,1)S(1)}, u32[]{:S(2)}, u32[]{:S(2)}) collective-permute-start(bf16[8,4096]{1,0:T(8,128)(2,1)S(1)} %add_convert_fusion.1), channel_id=1, source_target_pairs={{0,2},{1,3},{2,0},{3,1},{4,6},{5,7},{6,4},{7,5},{8,10},{9,11},{10,... | collective-permute-start | bytes 196616 | tf_op jit(solution)/shard_map/ppermute | solution.py:30
  74.8 8.0 %collective-permute-start.21 = (bf16[2,4096]{1,0:T(2,128)(2,1)S(1)}, bf16[2,4096]{1,0:T(2,128)(2,1)S(1)}, u32[]{:S(2)}, u32[]{:S(2)}) collective-permute-start(bf16[2,4096]{1,0:T(2,128)(2,1)S(1)} %get-tuple-element.42), channel_id=1, source_target_pairs={{0,4},{1,5},{2,6},{3,7},{4,0},{5,1},{6,2},{7,3},{8,12},{9,13},{10,... | collective-permute-start | bytes 49160 | tf_op jit(solution)/shard_map/ppermute | solution.py:30
  75.8 6.9 %collective-permute-start.23 = (bf16[2,4096]{1,0:T(2,128)(2,1)S(1)}, bf16[2,4096]{1,0:T(2,128)(2,1)S(1)}, u32[]{:S(2)}, u32[]{:S(2)}) collective-permute-start(bf16[2,4096]{1,0:T(2,128)(2,1)S(1)} %get-tuple-element.43), channel_id=1, source_target_pairs={{0,12},{1,13},{2,14},{3,15},{4,8},{5,9},{6,10},{7,11},{8,4},{9,5},... | collective-permute-start | bytes 49160 | tf_op jit(solution)/shard_map/ppermute | solution.py:30
  78.3 4.7 %collective-permute-start.22 = (bf16[2,4096]{1,0:T(2,128)(2,1)S(1)}, bf16[2,4096]{1,0:T(2,128)(2,1)S(1)}, u32[]{:S(2)}, u32[]{:S(2)}) collective-permute-start(bf16[2,4096]{1,0:T(2,128)(2,1)S(1)} %get-tuple-element.44), channel_id=1, source_target_pairs={{0,8},{1,9},{2,10},{3,11},{4,12},{5,13},{6,14},{7,15},{8,0},{9,1},... | collective-permute-start | bytes 49160 | tf_op jit(solution)/shard_map/ppermute | solution.py:30
  78.8 5.2 %collective-permute-start.9 = (bf16[8,4096]{1,0:T(8,128)(2,1)S(1)}, bf16[8,4096]{1,0:T(8,128)(2,1)S(1)}, u32[]{:S(2)}, u32[]{:S(2)}) collective-permute-start(bf16[8,4096]{1,0:T(8,128)(2,1)S(1)} %get-tuple-element.39), channel_id=1, source_target_pairs={{0,4},{1,5},{2,6},{3,7},{4,0},{5,1},{6,2},{7,3},{8,12},{9,13},{10,... | collective-permute-start | bytes 196616 | tf_op jit(solution)/shard_map/ppermute | solution.py:30
  80.3 6.2 %collective-permute-start.11 = (bf16[8,4096]{1,0:T(8,128)(2,1)S(1)}, bf16[8,4096]{1,0:T(8,128)(2,1)S(1)}, u32[]{:S(2)}, u32[]{:S(2)}) collective-permute-start(bf16[8,4096]{1,0:T(8,128)(2,1)S(1)} %get-tuple-element.40), channel_id=1, source_target_pairs={{0,12},{1,13},{2,14},{3,15},{4,8},{5,9},{6,10},{7,11},{8,4},{9,5},... | collective-permute-start | bytes 196616 | tf_op jit(solution)/shard_map/ppermute | solution.py:30
  82.7 5.5 %collective-permute-start.10 = (bf16[8,4096]{1,0:T(8,128)(2,1)S(1)}, bf16[8,4096]{1,0:T(8,128)(2,1)S(1)}, u32[]{:S(2)}, u32[]{:S(2)}) collective-permute-start(bf16[8,4096]{1,0:T(8,128)(2,1)S(1)} %get-tuple-element.41), channel_id=1, source_target_pairs={{0,8},{1,9},{2,10},{3,11},{4,12},{5,13},{6,14},{7,15},{8,0},{9,1},... | collective-permute-start | bytes 196616 | tf_op jit(solution)/shard_map/ppermute | solution.py:30
  (22 other events, 296.7 us)
